TPU v7x, 256 devices: a whole 4x4x8 slice. The times are simulated.
256 devices in a mesh: dp: 32 (over x, z), expert: 8 (over y, core).
Axes of the slice: x: 4, y: 4, z: 8, core: 2. Of those that a mesh axis runs over, the one named last changes fastest.
Arguments:
- tokens: bfloat16 [32768, 2048], P(('dp', 'expert')), may hold values from -24 to 24
- expert_ids: int32 [32768, 4], P(('dp', 'expert')), may hold values from 0 to 7, all different within a row; in each aligned block of 128 rows (0 to 127, 128 to 255, ...) at most 128 rows name the same one
- gates: bfloat16 [32768, 4], P(('dp', 'expert')), may hold values from 0.099609375 to 1
- w_gate: bfloat16 [8, 2048, 384], P('expert'), may hold values from -0.125 to 0.125
- w_up: bfloat16 [8, 2048, 384], P('expert'), may hold values from -0.125 to 0.125
- w_down: bfloat16 [8, 384, 2048], P('expert'), may hold values from -0.3125 to 0.3125
- cotangent: bfloat16 [32768, 2048], P(('dp', 'expert')), may hold values from -6 to 6
Outputs:
- mixed: bfloat16 [32768, 2048], P(('dp', 'expert'))
- grad_tokens: bfloat16 [32768, 2048], P(('dp', 'expert'))
- grad_gate: float32 [8, 2048, 384], P('expert', 'dp')
- grad_up: float32 [8, 2048, 384], P('expert', 'dp')
- grad_down: float32 [8, 384, 2048], P('expert', 'dp')
Inputs may be any that keep to these rules, and one draw needn't show every extreme that they name: `expert_ids`: each row names 4 different experts. In each aligned block of 128 rows (the rows of one device) no expert is named by more than 128 rows, a bound that some block reaches.
All inputs are finite; a program needn't handle non-finite values.
Results may differ from a plain program's by a relative error of at most 0.024.
Values may be sent and summed in bfloat16 or wider, within the bound.
A program may use at most 128 MiB of HBM per device.

v0:
```python
import jax
import jax.numpy as jnp
from jax import lax
from jax.sharding import PartitionSpec as P


def expert_rows(inputs, out_grads, gate_col, gate_panel, up_panel, down_panel):
    pre_gate = jnp.dot(inputs, gate_panel, preferred_element_type=jnp.float32)
    pre_up = jnp.dot(inputs, up_panel, preferred_element_type=jnp.float32)
    gate_sigmoid = jax.nn.sigmoid(pre_gate)
    activated = (pre_gate * gate_sigmoid * pre_up).astype(jnp.bfloat16)
    expert_out = jnp.dot(activated, down_panel, preferred_element_type=jnp.float32)
    contrib = (gate_col.astype(jnp.float32)[:, None] * expert_out).astype(jnp.bfloat16)
    act_grad = lax.dot_general(
        out_grads, down_panel, (((1,), (1,)), ((), ())), preferred_element_type=jnp.float32
    )
    up_grad = (act_grad * pre_gate * gate_sigmoid).astype(jnp.bfloat16)
    pre_grad = (act_grad * pre_up * gate_sigmoid * (1.0 + pre_gate * (1.0 - gate_sigmoid))).astype(
        jnp.bfloat16
    )
    grad_rows = lax.dot_general(
        pre_grad, gate_panel, (((1,), (1,)), ((), ())), preferred_element_type=jnp.float32
    )
    grad_rows = grad_rows + lax.dot_general(
        up_grad, up_panel, (((1,), (1,)), ((), ())), preferred_element_type=jnp.float32
    )
    grad_rows = grad_rows.astype(jnp.bfloat16)
    wgrad_gate = lax.dot_general(
        inputs, pre_grad, (((0,), (0,)), ((), ())), preferred_element_type=jnp.float32
    )
    wgrad_up = lax.dot_general(
        inputs, up_grad, (((0,), (0,)), ((), ())), preferred_element_type=jnp.float32
    )
    wgrad_down = lax.dot_general(
        activated, out_grads, (((0,), (0,)), ((), ())), preferred_element_type=jnp.float32
    )
    return (contrib, grad_rows, wgrad_gate, wgrad_up, wgrad_down)


def slot_table(route_ids, expert_num, per_source):
    token_count, pick_count = route_ids.shape
    matches = route_ids == expert_num
    hit_rows = jnp.any(matches, axis=1).astype(jnp.int32)
    which_pick = jnp.sum(
        matches.astype(jnp.int32) * jnp.arange(pick_count, dtype=jnp.int32)[None, :], axis=1
    )
    rank_of = jnp.cumsum(hit_rows) - hit_rows
    wanted = jnp.arange(per_source, dtype=jnp.int32)
    chosen = ((hit_rows[None, :] == 1) & (rank_of[None, :] == wanted[:, None])).astype(jnp.int32)
    valid_slot = jnp.sum(chosen, axis=1) > 0
    row_of = jnp.sum(chosen * jnp.arange(token_count, dtype=jnp.int32)[None, :], axis=1)
    pick_of = jnp.sum(chosen * which_pick[None, :], axis=1)
    return (row_of, pick_of, valid_slot)


def per_device(tokens, expert_ids, gates, w_gate, w_up, w_down, cotangent):
    tok_dev, model_width = tokens.shape
    group_size = lax.axis_size("expert")
    slot_count = group_size * tok_dev
    my_expert = lax.axis_index("expert")
    gate_panel = w_gate[0]
    up_panel = w_up[0]
    down_panel = w_down[0]
    all_rows, all_cot, all_gates = (
        lax.all_gather(tokens, "expert", axis=0, tiled=True),
        lax.all_gather(cotangent, "expert", axis=0, tiled=True),
        lax.all_gather(gates, "expert", axis=0, tiled=True),
    )
    all_ids = lax.all_gather(expert_ids, "expert", axis=0, tiled=True)
    source_ids = all_ids.reshape(group_size, tok_dev, all_ids.shape[1])
    row_of, pick_of, keep_mask = jax.vmap(
        lambda route_ids: slot_table(route_ids, my_expert, tok_dev)
    )(source_ids)
    flat_row = (row_of + jnp.arange(group_size, dtype=jnp.int32)[:, None] * tok_dev).reshape(
        slot_count
    )
    keep_b = keep_mask.reshape(slot_count).astype(jnp.bfloat16)
    inputs = all_rows[flat_row] * keep_b[:, None]
    gate_col = all_gates[flat_row, pick_of.reshape(slot_count)] * keep_b
    out_grads = (
        gate_col.astype(jnp.float32)[:, None] * all_cot[flat_row].astype(jnp.float32)
    ).astype(jnp.bfloat16)
    contrib, grad_rows, acc_gate, acc_up, acc_down = expert_rows(
        inputs, out_grads, gate_col, gate_panel, up_panel, down_panel
    )
    dest = jnp.where(keep_mask.reshape(slot_count), flat_row, group_size * tok_dev)
    part_out = (
        jnp.zeros((group_size * tok_dev, model_width), jnp.float32)
        .at[dest]
        .set(contrib.astype(jnp.float32), mode="drop")
    )
    part_grad = (
        jnp.zeros((group_size * tok_dev, model_width), jnp.float32)
        .at[dest]
        .set(grad_rows.astype(jnp.float32), mode="drop")
    )
    summed_out, summed_grad = (
        lax.psum_scatter(
            part_out.astype(jnp.bfloat16), "expert", scatter_dimension=0, tiled=True
        ).astype(jnp.float32),
        lax.psum_scatter(
            part_grad.astype(jnp.bfloat16), "expert", scatter_dimension=0, tiled=True
        ).astype(jnp.float32),
    )
    mixed = summed_out.astype(jnp.bfloat16)
    grad_tokens = summed_grad.astype(jnp.bfloat16)
    grad_gate, grad_up, grad_down = (
        lax.psum_scatter(
            acc_gate.astype(jnp.bfloat16), "dp", scatter_dimension=0, tiled=True
        ).astype(jnp.float32),
        lax.psum_scatter(acc_up.astype(jnp.bfloat16), "dp", scatter_dimension=0, tiled=True).astype(
            jnp.float32
        ),
        lax.psum_scatter(
            acc_down.astype(jnp.bfloat16), "dp", scatter_dimension=0, tiled=True
        ).astype(jnp.float32),
    )
    return (mixed, grad_tokens, grad_gate[None], grad_up[None], grad_down[None])


def solution(mesh):
    return jax.shard_map(
        per_device,
        mesh=mesh,
        in_specs=(
            P(("dp", "expert"), None),
            P(("dp", "expert"), None),
            P(("dp", "expert"), None),
            P("expert", None, None),
            P("expert", None, None),
            P("expert", None, None),
            P(("dp", "expert"), None),
        ),
        out_specs=(
            P(("dp", "expert"), None),
            P(("dp", "expert"), None),
            P("expert", "dp", None),
            P("expert", "dp", None),
            P("expert", "dp", None),
        ),
        check_vma=False,
    )
```

profile of v0, /device:TPU:1, one launch (start us, length us, event | category | flops | bytes accessed | tf_op | source)
XLA Modules:
  0.0 631.1 jit_solution(9545320917792145153)
XLA Ops:
  8.7 14.4 %all_gather.12 = s32[1024,4]{0,1:T(4,128)S(1)} all-gather(s32[128,4]{0,1:T(4,128)} %param.8), channel_id=1, replica_groups=mesh['dp'=32,'expert'=8] {'expert'}, dimensions={0}, use_global_device_ids=true | all-gather | bytes 18432 | tf_op jit(solution)/shard_map/all_gather | solution.py:69
  23.4 9.1 %all_gather.13 = bf16[1024,4]{0,1:T(4,128)(2,1)S(1)} all-gather(bf16[128,4]{0,1:T(4,128)(2,1)} %param.9), channel_id=1, replica_groups=mesh['dp'=32,'expert'=8] {'expert'}, dimensions={0}, use_global_device_ids=true | all-gather | bytes 9216 | tf_op jit(solution)/shard_map/all_gather | solution.py:67
  33.1 9.1 %gather_fusion = bf16[1024]{0:T(1024)(128)(2,1)S(1)} fusion(bf16[1024,4]{0,1:T(4,128)(2,1)S(1)} %all_gather.13, s32[1024]{0:T(1024)S(1)} %bitcast.63), kind=kCustom, calls=%fused_computation | custom fusion | bytes 12288 | tf_op jit(solution)/shard_map/gather | solution.py:79
  42.3 6.6 %all-gather.3.cloned.1.call-done = bf16[1024,2048]{1,0:T(8,128)(2,1)} async-done(((bf16[128,2048]{1,0:T(8,128)(2,1)}), bf16[1024,2048]{1,0:T(8,128)(2,1)}) %all-gather.3.cloned.1.call-update) | async-done | bytes 4194320 | tf_op jit(solution)/shard_map/all_gather | solution.py:65
  48.8 11.5 %gather_fusion.1 = bf16[1024,2048]{1,0:T(8,128)(2,1)} fusion(bf16[1024,2048]{1,0:T(8,128)(2,1)} %all-gather.3.cloned.1.call-done, s32[1024]{0:T(1024)S(1)} %broadcast_clamp_fusion), kind=kCustom, calls=%fused_computation.1 | custom fusion | bytes 8392704 | tf_op jit(solution)/shard_map/gather | solution.py:78
  60.4 6.7 %fusion.9 = f32[1024,384]{1,0:T(8,128)} fusion(bf16[1024,2048]{1,0:T(8,128)(2,1)} %gather_fusion.1, bf16[1024]{0:T(1024)(128)(2,1)S(1)} %bitcast_convert_fusion.2, bf16[1,2048,384]{2,1,0:T(8,128)(2,1)} %param.11), kind=kOutput, calls=%fused_computation.19 | convolution fusion | flops 1612709888 | bytes 7342080 | tf_op jit(solution)/shard_map/dot_general | solution.py:9
  70.7 14.7 %all-gather.5.cloned.1.call-done = bf16[1024,2048]{1,0:T(8,128)(2,1)} async-done(((bf16[128,2048]{1,0:T(8,128)(2,1)}), bf16[1024,2048]{1,0:T(8,128)(2,1)}) %all-gather.5.cloned.1.call-update) | async-done | bytes 4194320 | tf_op jit(solution)/shard_map/all_gather | solution.py:66
  85.4 11.5 %gather_fusion.2 = bf16[1024,2048]{1,0:T(8,128)(2,1)} fusion(bf16[1024,2048]{1,0:T(8,128)(2,1)} %all-gather.5.cloned.1.call-done, s32[1024]{0:T(1024)S(1)} %broadcast_clamp_fusion), kind=kCustom, calls=%fused_computation.2 | custom fusion | bytes 8392704 | tf_op jit(solution)/shard_map/gather | solution.py:81
  96.9 7.3 %multiply_convert_fusion.4 = (bf16[1024,384]{1,0:T(8,128)(2,1)S(1)}, bf16[1024,384]{1,0:T(8,128)(2,1)}, bf16[1024,384]{1,0:T(8,128)(2,1)}) fusion(f32[1024,384]{1,0:T(8,128)} %fusion.11, f32[1024,384]{1,0:T(8,128)} %fusion.9, bf16[1,384,2048]{2,1,0:T(8,128)(2,1)S(1)} %copy-done, bf16[1024,2048]{1,0:T(8,128)(2,1)} %gather_fusion.2, ...), kind=kOutput, calls=%fused_computation.35 | convolution fusion | flops 1623195648 | bytes 11276288 | tf_op jit(solution)/shard_map/dot_general | solution.py:14
  109.2 6.1 convolution_convert_fusion.2
  115.3 5.4 multiply_convert_fusion.1
  120.7 10.9 %scatter_custom_fusion = f32[1024,2048]{1,0:T(8,128)} fusion(s32[1024]{0:T(1024)S(1)} %bitcast.70, bf16[1024,2048]{1,0:T(8,128)(2,1)} %multiply_convert_fusion.1, f32[]{:T(128)} %constant.10.clone.1), kind=kCustom, calls=%fused_computation.9 | custom fusion | flops 2097152 | bytes 12582916 | tf_op jit(solution)/shard_map/scatter | solution.py:90
  131.7 6.0 convert_element_type.93
  141.7 4.3 add_convert_fusion
  146.0 10.9 %scatter_custom_fusion.1 = f32[1024,2048]{1,0:T(8,128)} fusion(s32[1024]{0:T(1024)S(1)} %bitcast.71, bf16[1024,2048]{1,0:T(8,128)(2,1)} %add_convert_fusion, f32[]{:T(128)} %constant.10.clone.1), kind=kCustom, calls=%fused_computation.5 | custom fusion | flops 2097152 | bytes 12582916 | tf_op jit(solution)/shard_map/scatter | solution.py:95
  156.9 6.0 convert_element_type.100
  163.0 4.4 convolution_convert_fusion
  167.4 75.8 %fusion = bf16[16,2048]{1,0:T(8,128)(2,1)S(1)} fusion(bf16[384,2048]{1,0:T(8,128)(2,1)S(1)} %convolution_convert_fusion), kind=kCustom, calls=%all-reduce-scatter | all-reduce-scatter fusion | flops 1048577 | bytes 1639424
  248.5 8.4 %collective-permute-start.3 = (bf16[16,2048]{1,0:T(8,128)(2,1)S(1)}, bf16[16,2048]{1,0:T(8,128)(2,1)S(1)}, u32[]{:S(2)}, u32[]{:S(2)}) collective-permute-start(bf16[16,2048]{1,0:T(8,128)(2,1)S(1)} %fusion), channel_id=1, source_target_pairs={{0,32},{8,40},{16,48},{24,56},{32,64},{40,72},{48,80},{56,88},{64,... | collective-permute-start | bytes 196616
  258.2 5.6 collective-permute-start.1
  270.4 49.4 %reduce-scatter.13.cloned.1.call-done = bf16[64,384]{1,0:T(8,128)(2,1)} async-done(((bf16[2048,384]{1,0:T(8,128)(2,1)}), bf16[64,384]{1,0:T(8,128)(2,1)}) %reduce-scatter.13.cloned.1.call-update) | async-done | bytes 49168 | tf_op jit(solution)/shard_map/reduce_scatter | solution.py:111
  321.3 216.4 %reduce-scatter.11.cloned.1.call-done = bf16[64,384]{1,0:T(8,128)(2,1)} async-done(((bf16[2048,384]{1,0:T(8,128)(2,1)}), bf16[64,384]{1,0:T(8,128)(2,1)}) %reduce-scatter.11.cloned.1.call-update) | async-done | bytes 49168 | tf_op jit(solution)/shard_map/reduce_scatter | solution.py:108
  539.1 42.9 %reduce-scatter.7.cloned.1.call-done = bf16[128,2048]{1,0:T(8,128)(2,1)} async-done(((bf16[1024,2048]{1,0:T(8,128)(2,1)}), bf16[128,2048]{1,0:T(8,128)(2,1)}) %reduce-scatter.7.cloned.1.call-update) | async-done | bytes 524304 | tf_op jit(solution)/shard_map/reduce_scatter | solution.py:98
  582.0 42.3 %reduce-scatter.9.cloned.1.call-done = bf16[128,2048]{1,0:T(8,128)(2,1)} async-done(((bf16[1024,2048]{1,0:T(8,128)(2,1)}), bf16[128,2048]{1,0:T(8,128)(2,1)}) %reduce-scatter.9.cloned.1.call-update) | async-done | bytes 524304 | tf_op jit(solution)/shard_map/reduce_scatter | solution.py:101
  (66 shorter events, 30.3 us)
Async XLA Ops:
  7.2 89.7 %copy-start = (bf16[1,384,2048]{2,1,0:T(8,128)(2,1)S(1)}, bf16[1,384,2048]{2,1,0:T(8,128)(2,1)}, u32[]{:S(2)}) copy-start(bf16[1,384,2048]{2,1,0:T(8,128)(2,1)} %param.12) | copy-start | bytes 4718596
  7.2 41.6 %all-gather.3.cloned.1.call-start = ((), (), s32[]{:S(2)}) async-start(), calls=%async_computation.4 | async-start | bytes 4718592 | tf_op jit(solution)/shard_map/all_gather | solution.py:65
  7.9 77.5 %all-gather.5.cloned.1.call-start = ((), (), s32[]{:S(2)}) async-start(), calls=%async_computation.6 | async-start | bytes 4718592 | tf_op jit(solution)/shard_map/all_gather | solution.py:66
  8.7 311.2 %reduce-scatter.13.cloned.1.call-start = ((), (), s32[]{:S(2)}) async-start(), calls=%async_computation.9 | async-start | bytes 1622016 | tf_op jit(solution)/shard_map/reduce_scatter | solution.py:111
  60.4 6.7 %copy-start.1 = (bf16[1024,2048]{1,0:T(8,128)(2,1)S(1)}, bf16[1024,2048]{1,0:T(8,128)(2,1)}, u32[]{:S(2)}) copy-start(bf16[1024,2048]{1,0:T(8,128)(2,1)} %gather_fusion.1) | copy-start | bytes 12582916
  60.4 6.7 %copy-start.3 = (bf16[1,2048,384]{2,1,0:T(8,128)(2,1)S(1)}, bf16[1,2048,384]{2,1,0:T(8,128)(2,1)}, u32[]{:S(2)}) copy-start(bf16[1,2048,384]{2,1,0:T(8,128)(2,1)} %param.10) | copy-start | bytes 4718596
  96.9 8.2 %copy-start.2 = (bf16[1024,2048]{1,0:T(8,128)(2,1)S(1)}, bf16[1024,2048]{1,0:T(8,128)(2,1)}, u32[]{:S(2)}) copy-start(bf16[1024,2048]{1,0:T(8,128)(2,1)} %gather_fusion.1) | copy-start | bytes 12582916
  104.2 0.9 copy-start.5
  108.9 428.7 %reduce-scatter.11.cloned.1.call-start = ((), (), s32[]{:S(2)}) async-start(), calls=%async_computation.8 | async-start | bytes 1622016 | tf_op jit(solution)/shard_map/reduce_scatter | solution.py:108
  115.3 466.7 %reduce-scatter.7.cloned.1.call-start = ((), (), s32[]{:S(2)}) async-start(), calls=%async_computation.5 | async-start | bytes 4718592 | tf_op jit(solution)/shard_map/reduce_scatter | solution.py:98
  137.7 486.6 %reduce-scatter.9.cloned.1.call-start = ((), (), s32[]{:S(2)}) async-start(), calls=%async_computation.7 | async-start | bytes 4718592 | tf_op jit(solution)/shard_map/reduce_scatter | solution.py:101
  138.0 3.7 copy-start.4
  138.0 3.7 copy-start.6
  163.0 103.9 %copy-start.7 = (u32[256]{0:T(256)S(1)}, u32[256]{0:T(256)}, u32[]{:S(2)}) copy-start(u32[256]{0:T(256)} %constant.53) | copy-start | bytes 3076
  243.3 14.9 %collective-permute-start.6 = (bf16[16,2048]{1,0:T(8,128)(2,1)S(1)}, bf16[16,2048]{1,0:T(8,128)(2,1)S(1)}, u32[]{:S(2)}, u32[]{:S(2)}) collective-permute-start(bf16[16,2048]{1,0:T(8,128)(2,1)S(1)} %fusion), channel_id=1, source_target_pairs={{0,56},{8,64},{16,72},{24,80},{32,88},{40,96},{48,104},{56,112},{6... | collective-permute-start | bytes 196616
  244.6 19.2 %collective-permute-start.5 = (bf16[16,2048]{1,0:T(8,128)(2,1)S(1)}, bf16[16,2048]{1,0:T(8,128)(2,1)S(1)}, u32[]{:S(2)}, u32[]{:S(2)}) collective-permute-start(bf16[16,2048]{1,0:T(8,128)(2,1)S(1)} %fusion), channel_id=1, source_target_pairs={{0,48},{8,56},{16,64},{24,72},{32,80},{40,88},{48,96},{56,104},{64... | collective-permute-start | bytes 196616
  245.9 11.0 %collective-permute-start.7 = (bf16[12,2048]{1,0:T(8,128)(2,1)S(1)}, bf16[12,2048]{1,0:T(8,128)(2,1)S(1)}, u32[]{:S(2)}, u32[]{:S(2)}) collective-permute-start(bf16[12,2048]{1,0:T(8,128)(2,1)S(1)} %slice.6), channel_id=1, source_target_pairs={{0,64},{8,72},{16,80},{24,88},{32,96},{40,104},{48,112},{56,120},{... | collective-permute-start | bytes 147464
  247.2 20.9 %collective-permute-start.4 = (bf16[16,2048]{1,0:T(8,128)(2,1)S(1)}, bf16[16,2048]{1,0:T(8,128)(2,1)S(1)}, u32[]{:S(2)}, u32[]{:S(2)}) collective-permute-start(bf16[16,2048]{1,0:T(8,128)(2,1)S(1)} %fusion), channel_id=1, source_target_pairs={{0,40},{8,48},{16,56},{24,64},{32,72},{40,80},{48,88},{56,96},{64,... | collective-permute-start | bytes 196616
  248.5 19.6 %collective-permute-start.3 = (bf16[16,2048]{1,0:T(8,128)(2,1)S(1)}, bf16[16,2048]{1,0:T(8,128)(2,1)S(1)}, u32[]{:S(2)}, u32[]{:S(2)}) collective-permute-start(bf16[16,2048]{1,0:T(8,128)(2,1)S(1)} %fusion), channel_id=1, source_target_pairs={{0,32},{8,40},{16,48},{24,56},{32,64},{40,72},{48,80},{56,88},{64,... | collective-permute-start | bytes 196616
  256.9 11.3 %collective-permute-start.2 = (bf16[16,2048]{1,0:T(8,128)(2,1)S(1)}, bf16[16,2048]{1,0:T(8,128)(2,1)S(1)}, u32[]{:S(2)}, u32[]{:S(2)}) collective-permute-start(bf16[16,2048]{1,0:T(8,128)(2,1)S(1)} %fusion), channel_id=1, source_target_pairs={{0,24},{8,32},{16,40},{24,48},{32,56},{40,64},{48,72},{56,80},{64,... | collective-permute-start | bytes 196616
  258.2 10.0 %collective-permute-start.1 = (bf16[16,2048]{1,0:T(8,128)(2,1)S(1)}, bf16[16,2048]{1,0:T(8,128)(2,1)S(1)}, u32[]{:S(2)}, u32[]{:S(2)}) collective-permute-start(bf16[16,2048]{1,0:T(8,128)(2,1)S(1)} %fusion), channel_id=1, source_target_pairs={{0,16},{8,24},{16,32},{24,40},{32,48},{40,56},{48,64},{56,72},{64,... | collective-permute-start | bytes 196616
  263.8 4.4 collective-permute-start
Sparse Core Ops, SparseCore 0:
  9.9 38.9 all-gather.2
  50.7 34.6 all-gather.4
  109.0 210.7 reduce-scatter.12
  323.5 214.1 reduce-scatter.10
  540.6 41.2 reduce-scatter.6
  585.0 39.3 reduce-scatter.8
where the time goes:
time: 634 us; the launch traced here: 631 us
  waiting for transfers between devices  374 us (59%)
  blocking collectives  99.3 us (16%)
  matrix products  45.2 us (7%)
  other arithmetic  37.8 us (6%)
  local copies, waits for them, and re-layouts  35.9 us (6%)
  starting transfers between devices  24.1 us (4%)
  between operations  15.1 us (2%)
    reduce_scatter x1, waiting for transfers between devices, per_device(): lax.psum_scatter(acc_gate.astype(jnp.bfloat16), 'dp', scatter_dimension=0...  216 us
    unnamed x1, blocking collectives  75.8 us
    reduce_scatter x1, waiting for transfers between devices, per_device(): lax.psum_scatter(acc_up.astype(jnp.bfloat16), 'dp', scatter_dimension=0,...  49.4 us
    reduce_scatter x1, waiting for transfers between devices, per_device(): lax.psum_scatter(part_out.astype(jnp.bfloat16), 'expert', scatter_dimensi...  42.9 us
    reduce_scatter x1, waiting for transfers between devices, per_device(): lax.psum_scatter(part_grad.astype(jnp.bfloat16), 'expert', scatter_dimens...  42.3 us
    unnamed x8, starting transfers between devices  23.5 us
    all_gather x1, waiting for transfers between devices, per_device(): lax.all_gather(cotangent, 'expert', axis=0, tiled=True)  14.7 us
    all_gather x1, blocking collectives, per_device(): all_ids = lax.all_gather(expert_ids, 'expert', axis=0, tiled=True)  14.4 us
  transfers between devices with their start and end apart: 14, of which 6 were waited for; matrix products, arithmetic and copies ran while one was open for 27% of the time, Pallas kernels for 0%

commit v1 on v0

v1 whole, which is shorter than its diff:
```python
import functools

import jax
import jax.numpy as jnp
from jax import lax
from jax.experimental import pallas as pl
from jax.experimental.pallas import tpu as pltpu
from jax.sharding import PartitionSpec as P

NX, NZ, NY = 4, 8, 4
F32 = jnp.float32
BF16 = jnp.bfloat16
NN = (((1,), (0,)), ((), ()))
NT = (((1,), (1,)), ((), ()))
TN = (((0,), (0,)), ((), ()))
COPIES = 96


def dot(a, b, dims=NN):
    return lax.dot_general(a, b, dims, preferred_element_type=F32)


def add_rows(dst, srcs):
    rows = dst.shape[-2]
    step = 16 if rows % 16 == 0 else rows

    if len(dst.shape) == 2:
        @pl.loop(0, rows // step)
        def _(i):
            sl = pl.ds(pl.multiple_of(i * step, step), step)
            total = dst[sl, :].astype(F32)
            for s in srcs:
                total = total + s[sl, :].astype(F32)
            dst[sl, :] = total.astype(dst.dtype)
    else:
        @pl.loop(0, dst.shape[0])
        def _(i):
            total = dst[i].astype(F32)
            for s in srcs:
                total = total + s[i].astype(F32)
            dst[i] = total.astype(dst.dtype)


def moe_kernel(
    tok, cot, ids_t, gates_t, wg, wu, wd,
    mixed, gtok, ggate, gup, gdown,
    X, C, G, OG, Wgu, Wd, O, SB, RY, PG, APT, PT, Ggu, Gd, RXg, RZgh, RZg, RZdh, RZd, RXd,
    load_sem, send_sem, recv_sem,
):
    T, D = tok.shape
    H = wg.shape[1]
    dp = lax.axis_index("dp")
    ex = lax.axis_index("expert")
    x, z = dp // NZ, dp % NZ
    y, core = ex // 2, ex % 2
    sib = (dp, y * 2 + (1 - core))
    yp = (dp, ((y + 1) % NY) * 2 + core)
    ym = (dp, ((y + NY - 1) % NY) * 2 + core)
    xp = (((x + 1) % NX) * NZ + z, ex)
    xm = (((x + NX - 1) % NX) * NZ + z, ex)
    zp = (x * NZ + (z + 1) % NZ, ex)
    zm = (x * NZ + (z + NZ - 1) % NZ, ex)

    copies = {}

    def reg(name, src, dst, dev):
        copies[name] = (len(copies), src, dst, dev)

    def desc(name):
        k, src, dst, dev = copies[name]
        return pltpu.make_async_remote_copy(
            src_ref=src, dst_ref=dst, send_sem=send_sem.at[k], recv_sem=recv_sem.at[k],
            device_id=dev, device_id_type=pl.DeviceIdType.MESH,
        )

    def start(*names):
        for n in names:
            desc(n).start()

    def recv(*names):
        for n in names:
            desc(n).wait_recv()

    for nm, buf in (("X", X), ("C", C), ("G", G)):
        reg(nm + "s0", buf.at[0, 0], buf.at[0, 1], sib)
        reg(nm + "p", buf.at[0, 0], buf.at[1, 0], yp)
        reg(nm + "m", buf.at[0, 0], buf.at[2, 0], ym)
        for i in (1, 2, 3):
            reg(nm + "s%d" % i, buf.at[i, 0], buf.at[i, 1], sib)
    reg("Xf", X.at[1, 0], X.at[3, 0], yp)
    reg("Gf", G.at[1, 0], G.at[3, 0], yp)
    reg("Cf", C.at[2, 0], C.at[3, 0], ym)
    for i in range(4):
        reg("O%d" % i, O.at[i, 1], SB.at[i], sib)

    def ring4(tag, a, b, r, plus, minus):
        reg(tag + "0", a(2), r(0), plus)
        reg(tag + "1", b(2), r(1), minus)
        reg(tag + "2", b(1), r(2), plus)
        reg(tag + "3", a(-1), r(3), minus)
        reg(tag + "4", a(1), r(4), plus)
        reg(tag + "5", b(-1), r(5), minus)

    def ring4_mid(tag, a, b, r):
        recv(tag + "0")
        add_rows(a(1), [r(0)])
        start(tag + "4")
        recv(tag + "1")
        add_rows(b(-1), [r(1)])
        start(tag + "5")

    slot_of = {0: 0, -1: 1, 1: 2, 2: 3}
    ya = lambda k: O.at[slot_of[k], 0, 0]
    yb = lambda k: O.at[slot_of[k], 0, 1]
    yr = lambda i: RY.at[i]
    ring4("y", ya, yb, yr, yp, ym)

    hz = NZ // 2
    ga = lambda k: Ggu.at[pl.ds(((x + k + NX) % NX) * NZ, hz)]
    gb = lambda k: Ggu.at[pl.ds(((x + k + NX) % NX) * NZ + hz, hz)]
    gr = lambda i: RXg.at[i]
    ring4("gx", ga, gb, gr, xp, xm)

    hd = D // 2
    da = lambda k: Gd.at[z, (x + k + NX) % NX, :, pl.ds(0, hd)]
    db = lambda k: Gd.at[z, (x + k + NX) % NX, :, pl.ds(hd, hd)]
    dr = lambda i: RXd.at[i]
    ring4("dx", da, db, dr, xp, xm)

    def ring8(tag, a, b, full, rh, r, plus, minus):
        reg(tag + "0", a(4), rh(0), plus)
        reg(tag + "1", b(4), rh(1), minus)
        for s, k in ((0, 3), (1, 2), (2, 1)):
            reg(tag + "p%d" % k, full(k), r(2 * s), plus)
            reg(tag + "m%d" % k, full(-k), r(2 * s + 1), minus)

    def ring8_first(tag, a, b, rh):
        recv(tag + "0")
        add_rows(a(3), [rh(0)])
        start(tag + "p3")
        recv(tag + "1")
        add_rows(b(-3), [rh(1)])
        start(tag + "m3")

    def ring8_mid(tag, full, r, k):
        s = 3 - k - 1
        recv(tag + "p%d" % (k + 1))
        add_rows(full(k), [r(2 * s)])
        start(tag + "p%d" % k)
        recv(tag + "m%d" % (k + 1))
        add_rows(full(-k), [r(2 * s + 1)])
        start(tag + "m%d" % k)

    hr = Ggu.shape[1] // 2
    sfull = lambda k: Ggu.at[x * NZ + (z + k + NZ) % NZ]
    sa = lambda k: Ggu.at[x * NZ + (z + k + NZ) % NZ, pl.ds(0, hr)]
    sb = lambda k: Ggu.at[x * NZ + (z + k + NZ) % NZ, pl.ds(hr, hr)]
    srh = lambda i: RZgh.at[i]
    sr = lambda i: RZg.at[i]
    ring8("gz", sa, sb, sfull, srh, sr, zp, zm)

    hx = NX // 2
    efull = lambda k: Gd.at[(z + k + NZ) % NZ]
    ea = lambda k: Gd.at[(z + k + NZ) % NZ, pl.ds(0, hx)]
    eb = lambda k: Gd.at[(z + k + NZ) % NZ, pl.ds(hx, hx)]
    erh = lambda i: RZdh.at[i]
    er = lambda i: RZd.at[i]
    ring8("dz", ea, eb, efull, erh, er, zp, zm)
    assert len(copies) <= COPIES

    loads = [
        pltpu.make_async_copy(tok, X.at[0, 0], load_sem.at[0]),
        pltpu.make_async_copy(cot, C.at[0, 0], load_sem.at[1]),
        pltpu.make_async_copy(wg, Wgu.at[:, pl.ds(0, H)], load_sem.at[2]),
        pltpu.make_async_copy(wu, Wgu.at[:, pl.ds(H, H)], load_sem.at[3]),
        pltpu.make_async_copy(wd, Wd, load_sem.at[4]),
    ]
    for cp in loads:
        cp.start()

    barrier = pltpu.get_barrier_semaphore()
    near = (sib, yp, ym, xp, xm, zp, zm)
    for dev in near:
        pl.semaphore_signal(barrier, inc=1, device_id=dev, device_id_type=pl.DeviceIdType.MESH)

    rows16 = lax.broadcasted_iota(jnp.int32, (16, T), 0)
    dense = jnp.zeros((16, T), F32)
    for k in range(ids_t.shape[0]):
        dense = dense + jnp.where(ids_t[k : k + 1, :] == rows16, gates_t[k : k + 1, :].astype(F32), 0.0)
    G[0, 0] = dense.astype(BF16)

    per = H // (NX * NZ)
    q = lax.broadcasted_iota(jnp.int32, PT.shape, 0)
    unit = lax.broadcasted_iota(jnp.int32, PT.shape, 1)
    j = q & 15
    wanted = (((q >> 4) & (NX - 1)) * NZ + (q >> 6)) * per + j
    PT[...] = jnp.where((unit == wanted) & (j < per), 1.0, 0.0).astype(BF16)

    pl.semaphore_wait(barrier, len(near))
    loads[0].wait()
    loads[1].wait()
    start("Xp", "Cm", "Gp", "Gm", "Gs0", "Xs0", "Cs0", "Cp", "Xm")
    for cp in loads[2:]:
        cp.wait()

    mine = (rows16 == ex).astype(F32).astype(BF16)

    def compute(i):
        gate = jnp.concatenate([dot(G[i, s], mine, TN)[:, :1] for s in (0, 1)], axis=0)
        rows = pl.ds(pl.multiple_of(i * 2 * T, 2 * T), 2 * T)
        inputs = X[i].reshape(2 * T, D)
        out_grad = (C[i].reshape(2 * T, D).astype(F32) * gate).astype(BF16)
        OG[rows, :] = out_grad
        pre = dot(inputs, Wgu[...])
        act_grad = dot(out_grad, Wd[...], NT)
        pre_gate, pre_up = pre[:, :H], pre[:, H:]
        sig = 1.0 / (1.0 + jnp.exp(-pre_gate))
        silu = pre_gate * sig
        activated = (silu * pre_up).astype(BF16)
        PG[rows, H:] = (act_grad * silu).astype(BF16)
        PG[rows, :H] = (act_grad * pre_up * sig * (1.0 + pre_gate * (1.0 - sig))).astype(BF16)
        APT[:, rows] = dot(PT[...], activated, NT).astype(BF16)

        @pl.loop(0, D // 512)
        def _(n):
            cols = pl.ds(pl.multiple_of(n * 512, 512), 512)
            part = (dot(activated, Wd[:, cols]) * gate).astype(BF16)
            grad = dot(PG[rows, :], Wgu[cols, :], NT).astype(BF16)
            for s in (0, 1):
                O[i, s, 0, :, cols] = part[s * T : (s + 1) * T]
                O[i, s, 1, :, cols] = grad[s * T : (s + 1) * T]

    def fold(i):
        recv("O%d" % i)
        for a in (0, 1):
            add_rows(O.at[i, 0, a], [SB.at[i, a]])

    def step(i, carry):
        @pl.when(i == 0)
        def _():
            recv("Xs0", "Cs0", "Gs0")

        @pl.when(i == 1)
        def _():
            recv("Xp", "Cm", "Gp", "Gm")
            start("Xf", "Cf", "Gf", "Gs1", "Gs2", "Xs1", "Cs2")
            recv("Cp", "Xm")
            start("Cs1", "Xs2")
            recv("Xs1", "Cs1", "Gs1")

        @pl.when(i == 2)
        def _():
            recv("Xs2", "Cs2", "Gs2")

        @pl.when(i == 3)
        def _():
            recv("Xf", "Cf", "Gf")
            start("Gs3", "Xs3", "Cs3")
            fold(1)
            start("y3")
            recv("Xs3", "Cs3", "Gs3")

        compute(i)
        for k in range(4):
            @pl.when(i == k)
            def _():
                start("O%d" % k)
        return carry

    lax.fori_loop(0, 4, step, 0)

    dims3 = (4, Ggu.shape[1], 2 * H)

    @pl.loop(0, D // 256)
    def _(m):
        cols = pl.ds(pl.multiple_of(m * 256, 256), 256)
        Ggu[pl.ds(m * 4, 4)] = (
            dot(X[:, :, :, cols].reshape(8 * T, 256), PG[...], TN).astype(BF16).reshape(dims3)
        )

    start("gx0", "gx1", "gx2", "gx3")
    fold(3)
    start("y0", "y1")
    fold(2)
    start("y2")

    @pl.loop(0, D // 512)
    def _(n):
        cols = pl.ds(pl.multiple_of(n * 512, 512), 512)
        Gd[:, :, :, cols] = dot(APT[...], OG[:, cols]).astype(BF16).reshape(NZ, NX, 16, 512)

    start("dz0", "dz1")
    fold(0)
    ring8_first("dz", ea, eb, erh)
    ring4_mid("gx", ga, gb, gr)
    ring8_mid("dz", efull, er, 2)
    ring4_mid("y", ya, yb, yr)
    ring8_mid("dz", efull, er, 1)
    recv("dzp1", "dzm1")
    add_rows(efull(0), [er(4), er(5)])
    start("dx0", "dx1", "dx2", "dx3")
    recv("gx3", "gx4")
    add_rows(ga(0), [gr(3), gr(4)])
    recv("gx2", "gx5")
    add_rows(gb(0), [gr(2), gr(5)])
    start("gz0", "gz1")
    ring4_mid("dx", da, db, dr)
    ring8_first("gz", sa, sb, srh)
    recv("y2", "y3", "y4", "y5")

    @pl.loop(0, T // 16)
    def _(i):
        sl = pl.ds(pl.multiple_of(i * 16, 16), 16)
        mixed[sl, :] = (
            O[0, 0, 0, sl, :].astype(F32) + RY[3, sl, :].astype(F32) + RY[4, sl, :].astype(F32)
        ).astype(BF16)
        gtok[sl, :] = (
            O[0, 0, 1, sl, :].astype(F32) + RY[2, sl, :].astype(F32) + RY[5, sl, :].astype(F32)
        ).astype(BF16)

    ring8_mid("gz", sfull, sr, 2)
    recv("dx2", "dx3", "dx4", "dx5")
    low = da(0)[...].astype(F32) + RXd[3].astype(F32) + RXd[4].astype(F32)
    high = db(0)[...].astype(F32) + RXd[2].astype(F32) + RXd[5].astype(F32)
    gdown[:, :hd] = low[:per]
    gdown[:, hd:] = high[:per]
    ring8_mid("gz", sfull, sr, 1)
    recv("gzp1", "gzm1")
    total = sfull(0)[...].astype(F32) + RZg[4].astype(F32) + RZg[5].astype(F32)
    ggate[...] = total[:, :H]
    gup[...] = total[:, H:]

    for n in copies:
        desc(n).wait_send()


def per_device(tokens, expert_ids, gates, w_gate, w_up, w_down, cotangent):
    T, D = tokens.shape
    H = w_gate.shape[2]
    rows = D // (NX * NZ)
    per = H // (NX * NZ)
    hbm = pl.BlockSpec(memory_space=pl.ANY)
    vmem = pl.BlockSpec(memory_space=pltpu.VMEM)
    V = pltpu.VMEM
    flops = 2 * 8 * T * D * H * 9
    mixed, gtok, ggate, gup, gdown = pl.pallas_call(
        moe_kernel,
        out_shape=(
            jax.ShapeDtypeStruct((T, D), BF16),
            jax.ShapeDtypeStruct((T, D), BF16),
            jax.ShapeDtypeStruct((rows, H), F32),
            jax.ShapeDtypeStruct((rows, H), F32),
            jax.ShapeDtypeStruct((per, D), F32),
        ),
        in_specs=[hbm, hbm, vmem, vmem, hbm, hbm, hbm],
        out_specs=(vmem,) * 5,
        scratch_shapes=[
            V((4, 2, T, D), BF16),
            V((4, 2, T, D), BF16),
            V((4, 2, 16, T), BF16),
            V((8 * T, D), BF16),
            V((D, 2 * H), BF16),
            V((H, D), BF16),
            V((4, 2, 2, T, D), BF16),
            V((4, 2, T, D), BF16),
            V((6, T, D), BF16),
            V((8 * T, 2 * H), BF16),
            V((NX * NZ * 16, 8 * T), BF16),
            V((NX * NZ * 16, H), BF16),
            V((NX * NZ, rows, 2 * H), BF16),
            V((NZ, NX, 16, D), BF16),
            V((6, NZ // 2, rows, 2 * H), BF16),
            V((2, rows // 2, 2 * H), BF16),
            V((6, rows, 2 * H), BF16),
            V((2, NX // 2, 16, D), BF16),
            V((6, NX, 16, D), BF16),
            V((6, 16, D // 2), BF16),
            pltpu.SemaphoreType.DMA((5,)),
            pltpu.SemaphoreType.DMA((COPIES,)),
            pltpu.SemaphoreType.DMA((COPIES,)),
        ],
        compiler_params=pltpu.CompilerParams(
            collective_id=0, has_side_effects=True, vmem_limit_bytes=60 * 2**20
        ),
        cost_estimate=pl.CostEstimate(flops=flops, bytes_accessed=32 << 20, transcendentals=8 * T * H),
        name="moe",
    )(tokens, cotangent, expert_ids.T, gates.T, w_gate[0], w_up[0], w_down[0])
    return mixed, gtok, ggate[None], gup[None], gdown[None]


def solution(mesh):
    return jax.shard_map(
        per_device,
        mesh=mesh,
        in_specs=(
            P(("dp", "expert"), None),
            P(("dp", "expert"), None),
            P(("dp", "expert"), None),
            P("expert", None, None),
            P("expert", None, None),
            P("expert", None, None),
            P(("dp", "expert"), None),
        ),
        out_specs=(
            P(("dp", "expert"), None),
            P(("dp", "expert"), None),
            P("expert", "dp", None),
            P("expert", "dp", None),
            P("expert", "dp", None),
        ),
        check_vma=False,
    )
```

time: 634 us -> 110 us (0.17)
  waiting for transfers between devices: 374 us -> 0 us
  Pallas kernels: 0 us -> 102 us
  blocking collectives: 99.3 us -> 0 us
  matrix products: 45.2 us -> 0 us
  other arithmetic: 37.8 us -> 0 us
  local copies, waits for them, and re-layouts: 35.9 us -> 5.68 us
  starting transfers between devices: 24.1 us -> 0 us
  between operations: 15.1 us -> 0.67 us
    reduce_scatter x4 -> x0, waiting for transfers between devices: 351 us -> none  [the longest x1 216 us: per_device(): lax.psum_scatter(acc_gate.astype(jnp.bfloat16), 'dp', scatter_dimension=0...]
    pallas_call x0 -> x1, Pallas kernels: none -> 102 us  [per_device(): pl.pallas_call(moe_kernel, out_shape=(jax.ShapeDtypeStruct((T, D), BF16),...]
    unnamed x1 -> x0, blocking collectives: 75.8 us -> none
    dot_general x9 -> x0, matrix products: 45.2 us -> none  [the longest x1 7.32 us: expert_rows(): lax.dot_general(out_grads, down_panel, (((1,), (1,)), ((), ())), preferre...]
    gather x3 -> x0, local copies, waits for them, and re-layouts: 32.1 us -> none  [the longest x1 11.5 us: per_device(): inputs = all_rows[flat_row] * keep_b[:, None]]
    unnamed x8 -> x0, starting transfers between devices: 23.5 us -> none
    all_gather x2 -> x0, blocking collectives: 23.5 us -> none  [the longest x1 14.4 us: per_device(): all_ids = lax.all_gather(expert_ids, 'expert', axis=0, tiled=True)]
    scatter x2 -> x0, other arithmetic: 21.9 us -> none  [the longest x1 10.9 us: per_device(): part_grad = jnp.zeros((group_size * tok_dev, model_width), jnp.float32).a...]
  transfers between devices with their start and end apart: 14 -> 0, of which waited for: 6 -> 0; matrix products, arithmetic and copies ran while one was open for 27% -> 0% of each run, Pallas kernels for 0% -> 0%
where the time goes in v1:
time: 110 us; the launch traced here: 108 us
  Pallas kernels  102 us (93%)
  local copies, waits for them, and re-layouts  5.68 us (5%)
    pallas_call x1, Pallas kernels, per_device(): pl.pallas_call(moe_kernel, out_shape=(jax.ShapeDtypeStruct((T, D), BF16),...  102 us
    unnamed x11, local copies, waits for them, and re-layouts  5.68 us

profile of v1, /device:TPU:1, one launch (start us, length us, event | category | flops | bytes accessed | tf_op | source)
XLA Modules:
  0.0 108.3 jit_solution(5308732009800287564)
XLA Ops:
  0.6 102.0 %moe.1 = (bf16[128,2048]{1,0:T(8,128)(2,1)}, bf16[128,2048]{1,0:T(8,128)(2,1)}, f32[64,384]{1,0:T(8,128)}, f32[64,384]{1,0:T(8,128)}, f32[12,2048]{1,0:T(8,128)}) custom-call(bf16[128,2048]{1,0:T(8,128)(2,1)} %tok.1, bf16[128,2048]{1,0:T(8,128)(2,1)} %cot.1, s32[4,128]{1,0:T(4,128)} %bitcast.14, bf16[4,128]{1,0:T(4,128)(2,1)} %bitcast.15, ...), custom_call_target="tpu_custom_call" | custom-call | flops 14495514624 | bytes 33554432 | tf_op jit(solution)/shard_map/moe/pallas_call | solution.py:346
  102.6 0.0 copy-start
  102.7 0.0 copy-start.2
  102.7 0.0 copy-start.1
  102.7 1.7 %copy.12 = f32[1,12,2048]{2,0,1:T(1,128)} copy(f32[1,12,2048]{2,1,0:T(8,128)} %bitcast.8) | data formatting | bytes 196608
  104.4 1.9 %copy.17 = bf16[128,2048]{1,0:T(8,128)(2,1)} copy(bf16[128,2048]{1,0:T(8,128)(2,1)} %get-tuple-element.25) | data formatting | bytes 1048576
  106.3 0.0 copy-done
  106.3 0.8 copy.18
  107.1 0.0 copy-done.2
  107.1 0.6 copy.19
  107.7 0.0 copy-done.1
  107.7 0.6 copy.20
Async XLA Ops:
  102.6 3.6 %copy-start = (bf16[128,2048]{1,0:T(8,128)(2,1)S(1)}, bf16[128,2048]{1,0:T(8,128)(2,1)}, u32[]{:S(2)}) copy-start(bf16[128,2048]{1,0:T(8,128)(2,1)} %get-tuple-element.26) | copy-start | bytes 1572868
  102.7 4.4 %copy-start.2 = (f32[64,384]{1,0:T(8,128)S(1)}, f32[64,384]{1,0:T(8,128)}, u32[]{:S(2)}) copy-start(f32[64,384]{1,0:T(8,128)} %get-tuple-element.12) | copy-start | bytes 294916
  102.7 5.0 %copy-start.1 = (f32[64,384]{1,0:T(8,128)S(1)}, f32[64,384]{1,0:T(8,128)}, u32[]{:S(2)}) copy-start(f32[64,384]{1,0:T(8,128)} %get-tuple-element.13) | copy-start | bytes 294916

commit v2 on v1

v2 whole, which is shorter than its diff:
```python
import functools

import jax
import jax.numpy as jnp
from jax import lax
from jax.experimental import pallas as pl
from jax.experimental.pallas import tpu as pltpu
from jax.sharding import PartitionSpec as P

NX, NZ, NY = 4, 8, 4
F32 = jnp.float32
BF16 = jnp.bfloat16
NN = (((1,), (0,)), ((), ()))
NT = (((1,), (1,)), ((), ()))
TN = (((0,), (0,)), ((), ()))
COPIES = 96


def dot(a, b, dims=NN):
    return lax.dot_general(a, b, dims, preferred_element_type=F32)


def add_rows(dst, srcs):
    rows = dst.shape[-2]
    step = 16 if rows % 16 == 0 else rows

    if len(dst.shape) == 2:
        @pl.loop(0, rows // step)
        def _(i):
            sl = pl.ds(pl.multiple_of(i * step, step), step)
            total = dst[sl, :].astype(F32)
            for s in srcs:
                total = total + s[sl, :].astype(F32)
            dst[sl, :] = total.astype(dst.dtype)
    else:
        @pl.loop(0, dst.shape[0])
        def _(i):
            total = dst[i].astype(F32)
            for s in srcs:
                total = total + s[i].astype(F32)
            dst[i] = total.astype(dst.dtype)


def moe_kernel(
    tok, cot, ids_t, gates_t, wg, wu, wd,
    mixed, gtok, ggate, gup, gdown,
    X, C, G, OG, Wgu, Wd, O, SB, RY, PG, ACT, GC, APT, PT, GACC, DACC,
    S1, S2, S3, S3x, R1, R1h, R1z, R2h, R2z, R2x, R3h, R3z, R3x,
    load_sem, send_sem, recv_sem,
):
    T, D = tok.shape
    H = wg.shape[1]
    CX = S1.shape[3]
    per = H // (NX * NZ)
    dp = lax.axis_index("dp")
    ex = lax.axis_index("expert")
    x, z = dp // NZ, dp % NZ
    y, core = ex // 2, ex % 2
    sib = (dp, y * 2 + (1 - core))
    yp = (dp, ((y + 1) % NY) * 2 + core)
    ym = (dp, ((y + NY - 1) % NY) * 2 + core)
    xp = (((x + 1) % NX) * NZ + z, ex)
    xm = (((x + NX - 1) % NX) * NZ + z, ex)
    zp = (x * NZ + (z + 1) % NZ, ex)
    zm = (x * NZ + (z + NZ - 1) % NZ, ex)
    at_x = lambda k: (x + k + NX) % NX
    at_z = lambda k: (z + k + NZ) % NZ

    copies = {}

    def reg(name, src, dst, dev):
        copies[name] = (len(copies), src, dst, dev)

    def desc(name):
        k, src, dst, dev = copies[name]
        return pltpu.make_async_remote_copy(
            src_ref=src, dst_ref=dst, send_sem=send_sem.at[k], recv_sem=recv_sem.at[k],
            device_id=dev, device_id_type=pl.DeviceIdType.MESH,
        )

    def start(*names):
        for n in names:
            desc(n).start()

    def recv(*names):
        for n in names:
            desc(n).wait_recv()

    for nm, buf in (("X", X), ("C", C), ("G", G)):
        reg(nm + "s0", buf.at[0, 0], buf.at[0, 1], sib)
        reg(nm + "p", buf.at[0, 0], buf.at[1, 0], yp)
        reg(nm + "m", buf.at[0, 0], buf.at[2, 0], ym)
        for i in (1, 2, 3):
            reg(nm + "s%d" % i, buf.at[i, 0], buf.at[i, 1], sib)
    reg("Xf", X.at[1, 0], X.at[3, 0], yp)
    reg("Gf", G.at[1, 0], G.at[3, 0], yp)
    reg("Cf", C.at[2, 0], C.at[3, 0], ym)
    for i in range(4):
        reg("O%d" % i, O.at[i, 1], SB.at[i], sib)

    def ring4(tag, a, b, r, plus, minus):
        reg(tag + "0", a(2), r(0), plus)
        reg(tag + "1", b(2), r(1), minus)
        reg(tag + "2", b(1), r(2), plus)
        reg(tag + "3", a(-1), r(3), minus)
        reg(tag + "4", a(1), r(4), plus)
        reg(tag + "5", b(-1), r(5), minus)

        def mid():
            recv(tag + "0")
            add_rows(a(1), [r(0)])
            start(tag + "4")
            recv(tag + "1")
            add_rows(b(-1), [r(1)])
            start(tag + "5")

        return mid

    def ring8(tag, a, b, full, rh, r, plus, minus):
        reg(tag + "0", a(4), rh(0), plus)
        reg(tag + "1", b(4), rh(1), minus)
        for s, k in ((0, 3), (1, 2), (2, 1)):
            reg(tag + "p%d" % k, full(k), r(2 * s), plus)
            reg(tag + "m%d" % k, full(-k), r(2 * s + 1), minus)

        def hop(k):
            if k == 3:
                recv(tag + "0")
                add_rows(a(3), [rh(0)])
                start(tag + "p3")
                recv(tag + "1")
                add_rows(b(-3), [rh(1)])
                start(tag + "m3")
                return
            s = 2 - k
            recv(tag + "p%d" % (k + 1))
            add_rows(full(k), [r(2 * s)])
            start(tag + "p%d" % k)
            recv(tag + "m%d" % (k + 1))
            add_rows(full(-k), [r(2 * s + 1)])
            start(tag + "m%d" % k)

        return hop

    slot_of = {0: 0, -1: 1, 1: 2, 2: 3}
    HT = T // 2
    y_mid = []
    for p in (0, 1):
        piece = pl.ds(p * HT, HT)
        y_mid.append(ring4(
            "y%d" % p,
            lambda k, piece=piece: O.at[slot_of[k], 0, 0, piece],
            lambda k, piece=piece: O.at[slot_of[k], 0, 1, piece],
            lambda i, piece=piece: RY.at[i, piece],
            yp, ym,
        ))

    hz = NZ // 2
    a1 = lambda k: S1.at[at_x(k), pl.ds(0, hz)]
    b1 = lambda k: S1.at[at_x(k), pl.ds(hz, hz)]
    r1 = lambda i: R1.at[i]
    s1_mid = ring4("s1x", a1, b1, r1, xp, xm)
    rows = S1.shape[2]
    hr = rows // 2
    f1z = lambda k: S1.at[x, at_z(k)]
    s1_hop = ring8(
        "s1z",
        lambda k: S1.at[x, at_z(k), pl.ds(0, hr)],
        lambda k: S1.at[x, at_z(k), pl.ds(hr, hr)],
        f1z, lambda i: R1h.at[i], lambda i: R1z.at[i], zp, zm,
    )

    hx = NX // 2
    f2 = lambda k: S2.at[at_z(k)]
    s2_hop = ring8(
        "s2z",
        lambda k: S2.at[at_z(k), pl.ds(0, hx)],
        lambda k: S2.at[at_z(k), pl.ds(hx, hx)],
        f2, lambda i: R2h.at[i], lambda i: R2z.at[i], zp, zm,
    )
    a2 = lambda k: S2.at[z, at_x(k), pl.ds(0, hr)]
    b2 = lambda k: S2.at[z, at_x(k), pl.ds(hr, hr)]
    s2_mid = ring4("s2x", a2, b2, lambda i: R2x.at[i], xp, xm)

    hd = D // 2
    f3 = lambda k: S3.at[at_z(k)]
    s3_hop = ring8(
        "s3z",
        lambda k: S3.at[at_z(k), :, pl.ds(0, hd)],
        lambda k: S3.at[at_z(k), :, pl.ds(hd, hd)],
        f3, lambda i: R3h.at[i], lambda i: R3z.at[i], zp, zm,
    )
    a3 = lambda k: S3x.at[at_x(k), :, pl.ds(0, hd)]
    b3 = lambda k: S3x.at[at_x(k), :, pl.ds(hd, hd)]
    s3_mid = ring4("s3x", a3, b3, lambda i: R3x.at[i], xp, xm)
    assert len(copies) <= COPIES

    loads = [
        pltpu.make_async_copy(tok, X.at[0, 0], load_sem.at[0]),
        pltpu.make_async_copy(cot, C.at[0, 0], load_sem.at[1]),
        pltpu.make_async_copy(wg, Wgu.at[:, pl.ds(0, H)], load_sem.at[2]),
        pltpu.make_async_copy(wu, Wgu.at[:, pl.ds(H, H)], load_sem.at[3]),
        pltpu.make_async_copy(wd, Wd, load_sem.at[4]),
    ]
    for cp in loads:
        cp.start()

    barrier = pltpu.get_barrier_semaphore()
    near = (sib, yp, ym, xp, xm, zp, zm)
    for dev in near:
        pl.semaphore_signal(barrier, inc=1, device_id=dev, device_id_type=pl.DeviceIdType.MESH)

    rows16 = lax.broadcasted_iota(jnp.int32, (16, T), 0)
    dense = jnp.zeros((16, T), F32)
    for k in range(ids_t.shape[0]):
        dense = dense + jnp.where(ids_t[k : k + 1, :] == rows16, gates_t[k : k + 1, :].astype(F32), 0.0)
    G[0, 0] = dense.astype(BF16)

    loads[0].wait()
    loads[1].wait()
    pl.semaphore_wait(barrier, len(near))
    start("Xp", "Cm", "Gp", "Gm", "Gs0", "Xs0", "Cs0", "Cp", "Xm")

    q = lax.broadcasted_iota(jnp.int32, PT.shape, 0)
    unit = lax.broadcasted_iota(jnp.int32, PT.shape, 1)
    row = ((unit // per) % NZ) * (NX * per) + (unit // (per * NZ)) * per + unit % per
    PT[...] = jnp.where(q == row, 1.0, 0.0).astype(BF16)

    for cp in loads[2:]:
        cp.wait()

    mine = (rows16 == ex).astype(F32).astype(BF16)

    def rows_of(i):
        return pl.ds(pl.multiple_of(i * 2 * T, 2 * T), 2 * T)

    def hidden(i):
        gate = jnp.concatenate([dot(G[i, s], mine, TN) for s in (0, 1)], axis=0)
        GC[...] = gate
        gate = gate[:, :1]
        here = rows_of(i)
        inputs = X[i].reshape(2 * T, D)
        out_grad = (C[i].reshape(2 * T, D).astype(F32) * gate).astype(BF16)
        OG[here, :] = out_grad
        pre = dot(inputs, Wgu[...])
        act_grad = dot(out_grad, Wd[...], NT)
        pre_gate, pre_up = pre[:, :H], pre[:, H:]
        sig = 1.0 / (1.0 + jnp.exp(-pre_gate))
        silu = pre_gate * sig
        activated = (silu * pre_up).astype(BF16)
        ACT[...] = activated
        PG[here, H:] = (act_grad * silu).astype(BF16)
        PG[here, :H] = (act_grad * pre_up * sig * (1.0 + pre_gate * (1.0 - sig))).astype(BF16)
        APT[:, here] = dot(PT[...], activated, NT).astype(BF16)

    def outputs(i):
        @pl.loop(0, D // 512)
        def _(n):
            cols = pl.ds(pl.multiple_of(n * 512, 512), 512)
            part = (dot(ACT[...], Wd[:, cols]) * GC[:, :1]).astype(BF16)
            grad = dot(PG[rows_of(i), :], Wgu[cols, :], NT).astype(BF16)
            for s in (0, 1):
                O[i, s, 0, :, cols] = part[s * T : (s + 1) * T]
                O[i, s, 1, :, cols] = grad[s * T : (s + 1) * T]

    def gate_up_part(m, first, count):
        cols = pl.ds(pl.multiple_of(m * 256, 256), 256)
        span = pl.ds(first * 2 * T, count * 2 * T)
        return dot(X[pl.ds(first, count), :, :, cols].reshape(count * 2 * T, 256), PG[span, :], TN)

    def down_part(n, first, count):
        cols = pl.ds(pl.multiple_of(n * 512, 512), 512)
        span = pl.ds(first * 2 * T, count * 2 * T)
        return dot(APT[:, span], OG[span, cols])

    def partial(first, count, fresh):
        @pl.loop(0, D // 256)
        def _(m):
            here = pl.ds(pl.multiple_of(m * 256, 256), 256)
            new = gate_up_part(m, first, count)
            GACC[here, :] = new if fresh else GACC[here, :] + new

        @pl.loop(0, D // 512)
        def _(n):
            cols = pl.ds(pl.multiple_of(n * 512, 512), 512)
            new = down_part(n, first, count)
            DACC[:, cols] = new if fresh else DACC[:, cols] + new

    def finish():
        @pl.loop(0, D // 512)
        def _(n):
            cols = pl.ds(pl.multiple_of(n * 512, 512), 512)
            S3[:, :, cols] = (DACC[:, cols] + down_part(n, 3, 1)).astype(BF16).reshape(NZ, NX * per, 512)

        start("s3z0", "s3z1")

        @pl.loop(0, 8)
        def _(t):
            k = t // 2
            xx = (x + jnp.where(k == 0, 2, jnp.where(k == 1, 1, jnp.where(k == 2, 3, 0)))) % NX
            half = t % 2
            m = xx * 2 + half
            here = pl.ds(pl.multiple_of(m * 256, 256), 256)
            new = (GACC[here, :] + gate_up_part(m, 3, 1)).astype(BF16)
            S1[xx, pl.ds(half * hz, hz)] = new[:, :CX].reshape(hz, rows, CX)
            S2[pl.ds(half * hz, hz), xx] = new[:, CX:].reshape(hz, rows, 2 * H - CX)
            for at, name in ((0, "s1x0"), (1, "s1x1"), (3, "s1x2"), (4, "s1x3")):
                @pl.when(t == at)
                def _():
                    start(name)

        start("s2z0", "s2z1")

    def fold(i):
        recv("O%d" % i)
        for a in (0, 1):
            add_rows(O.at[i, 0, a], [SB.at[i, a]])

    def step(i, carry):
        @pl.when(i == 0)
        def _():
            recv("Xs0", "Cs0", "Gs0")

        @pl.when(i == 1)
        def _():
            partial(0, 1, True)
            recv("Xp", "Cm", "Gp", "Gm")
            start("Xf", "Cf", "Gf", "Gs1", "Gs2", "Xs1", "Cs2")
            recv("Cp", "Xm")
            start("Cs1", "Xs2")
            recv("Xs1", "Cs1", "Gs1")

        @pl.when(i == 2)
        def _():
            recv("Xs2", "Cs2", "Gs2")

        @pl.when(i == 3)
        def _():
            fold(1)
            start("y03", "y13")
            fold(2)
            start("y02", "y12")
            recv("Xf", "Cf", "Gf")
            start("Gs3", "Xs3", "Cs3")
            partial(1, 2, False)
            recv("Xs3", "Cs3", "Gs3")

        hidden(i)

        @pl.when(i == 3)
        def _():
            finish()

        outputs(i)
        for k in range(4):
            @pl.when(i == k)
            def _():
                start("O%d" % k)
        return carry

    lax.fori_loop(0, 4, step, 0)

    def y_final(p):
        recv("y%d2" % p, "y%d3" % p, "y%d4" % p, "y%d5" % p)

        @pl.loop(0, HT // 16)
        def _(i):
            sl = pl.ds(pl.multiple_of(p * HT + i * 16, 16), 16)
            mixed[sl, :] = (
                O[0, 0, 0, sl, :].astype(F32) + RY[3, sl, :].astype(F32) + RY[4, sl, :].astype(F32)
            ).astype(BF16)
            gtok[sl, :] = (
                O[0, 0, 1, sl, :].astype(F32) + RY[2, sl, :].astype(F32) + RY[5, sl, :].astype(F32)
            ).astype(BF16)

    s3_hop(3)
    fold(3)
    start("y00", "y01", "y10", "y11")
    s2_hop(3)
    s1_mid()
    fold(0)
    s3_hop(2)
    s2_hop(2)
    y_mid[0]()
    s3_hop(1)
    recv("s1x3", "s1x4")
    add_rows(a1(0), [r1(3), r1(4)])
    recv("s1x2", "s1x5")
    add_rows(b1(0), [r1(2), r1(5)])
    start("s1z0", "s1z1")
    y_mid[1]()
    s2_hop(1)
    s1_hop(3)

    recv("s3zp1", "s3zm1")
    p_row = lax.broadcasted_iota(jnp.int32, (NX * 16, NX * per), 0)
    p_unit = lax.broadcasted_iota(jnp.int32, (NX * 16, NX * per), 1)
    apart = jnp.where(p_row == (p_unit // per) * 16 + p_unit % per, 1.0, 0.0).astype(BF16)

    @pl.loop(0, D // 512)
    def _(n):
        cols = pl.ds(pl.multiple_of(n * 512, 512), 512)
        total = S3[z, :, cols].astype(F32) + R3z[4, :, cols].astype(F32) + R3z[5, :, cols].astype(F32)
        S3x[:, :, cols] = dot(apart, total.astype(BF16)).astype(BF16).reshape(NX, 16, 512)

    start("s3x0", "s3x1", "s3x2", "s3x3")
    s1_hop(2)
    recv("s2zp1", "s2zm1")
    add_rows(f2(0), [R2z.at[4], R2z.at[5]])
    start("s2x0", "s2x1", "s2x2", "s2x3")
    s3_mid()
    y_final(0)
    s1_hop(1)
    s2_mid()
    recv("s3x2", "s3x3", "s3x4", "s3x5")
    low = a3(0)[...].astype(F32) + R3x[3].astype(F32) + R3x[4].astype(F32)
    high = b3(0)[...].astype(F32) + R3x[2].astype(F32) + R3x[5].astype(F32)
    for j in range(per):
        gdown[j, :, :hd] = low[j : j + 1]
        gdown[j, :, hd:] = high[j : j + 1]
    y_final(1)
    recv("s2x2", "s2x3", "s2x4", "s2x5")
    gup[:hr, CX - H :] = a2(0)[...].astype(F32) + R2x[3].astype(F32) + R2x[4].astype(F32)
    gup[hr:, CX - H :] = b2(0)[...].astype(F32) + R2x[2].astype(F32) + R2x[5].astype(F32)
    recv("s1zp1", "s1zm1")
    total = f1z(0)[...].astype(F32) + R1z[4].astype(F32) + R1z[5].astype(F32)
    ggate[...] = total[:, :H]
    gup[:, : CX - H] = total[:, H:]

    for n in copies:
        desc(n).wait_send()


def copy_kernel(*refs):
    half = len(refs) // 2
    for k in range(half):
        refs[half + k][...] = refs[k][...]


def per_device(tokens, expert_ids, gates, w_gate, w_up, w_down, cotangent):
    T, D = tokens.shape
    H = w_gate.shape[2]
    rows = D // (NX * NZ)
    per = H // (NX * NZ)
    hbm = pl.BlockSpec(memory_space=pl.ANY)
    vmem = pl.BlockSpec(memory_space=pltpu.VMEM)
    V = pltpu.VMEM
    CX = 512
    CZ = 2 * H - CX
    flops = 2 * 8 * T * D * H * 9
    shapes = (
        jax.ShapeDtypeStruct((T, D), BF16),
        jax.ShapeDtypeStruct((T, D), BF16),
        jax.ShapeDtypeStruct((rows, H), F32),
        jax.ShapeDtypeStruct((rows, H), F32),
        jax.ShapeDtypeStruct((per, 1, D), F32),
    )
    outs = pl.pallas_call(
        moe_kernel,
        out_shape=shapes,
        in_specs=[hbm, hbm, vmem, vmem, hbm, hbm, hbm],
        out_specs=(vmem,) * 5,
        scratch_shapes=[
            V((4, 2, T, D), BF16),
            V((4, 2, T, D), BF16),
            V((4, 2, 16, T), BF16),
            V((8 * T, D), BF16),
            V((D, 2 * H), BF16),
            V((H, D), BF16),
            V((4, 2, 2, T, D), BF16),
            V((4, 2, T, D), BF16),
            V((6, T, D), BF16),
            V((8 * T, 2 * H), BF16),
            V((2 * T, H), BF16),
            V((2 * T, 128), F32),
            V((H, 8 * T), BF16),
            V((H, H), BF16),
            V((D, 2 * H), F32),
            V((H, D), F32),
            V((NX, NZ, rows, CX), BF16),
            V((NZ, NX, rows, CZ), BF16),
            V((NZ, NX * per, D), BF16),
            V((NX, 16, D), BF16),
            V((6, NZ // 2, rows, CX), BF16),
            V((2, rows // 2, CX), BF16),
            V((6, rows, CX), BF16),
            V((2, NX // 2, rows, CZ), BF16),
            V((6, NX, rows, CZ), BF16),
            V((6, rows // 2, CZ), BF16),
            V((2, NX * per, D // 2), BF16),
            V((6, NX * per, D), BF16),
            V((6, 16, D // 2), BF16),
            pltpu.SemaphoreType.DMA((5,)),
            pltpu.SemaphoreType.DMA((COPIES,)),
            pltpu.SemaphoreType.DMA((COPIES,)),
        ],
        compiler_params=pltpu.CompilerParams(
            collective_id=0, has_side_effects=True, vmem_limit_bytes=63 * 2**20
        ),
        cost_estimate=pl.CostEstimate(flops=flops, bytes_accessed=32 << 20, transcendentals=8 * T * H),
        name="moe",
    )(tokens, cotangent, expert_ids.T, gates.T, w_gate[0], w_up[0], w_down[0])
    mixed, gtok, ggate, gup, gdown = pl.pallas_call(
        copy_kernel,
        out_shape=shapes,
        in_specs=[vmem] * 5,
        out_specs=(vmem,) * 5,
        name="hand_out",
    )(*outs)
    return mixed, gtok, ggate[None], gup[None], gdown.reshape(1, per, D)


def solution(mesh):
    return jax.shard_map(
        per_device,
        mesh=mesh,
        in_specs=(
            P(("dp", "expert"), None),
            P(("dp", "expert"), None),
            P(("dp", "expert"), None),
            P("expert", None, None),
            P("expert", None, None),
            P("expert", None, None),
            P(("dp", "expert"), None),
        ),
        out_specs=(
            P(("dp", "expert"), None),
            P(("dp", "expert"), None),
            P("expert", "dp", None),
            P("expert", "dp", None),
            P("expert", "dp", None),
        ),
        check_vma=False,
    )
```

time: 110 us -> 96.8 us (0.88); the launches traced: 108 us -> 96.6 us
  Pallas kernels: 102 us -> 96 us
  local copies, waits for them, and re-layouts: 5.68 us -> 0 us
    pallas_call x1 -> x2, Pallas kernels: 102 us -> 96 us  [the longest x1 93.6 us: per_device(): pl.pallas_call(moe_kernel, out_shape=shapes, in_specs=[hbm, hbm, vmem, vm...]
    unnamed x11 -> x0, local copies, waits for them, and re-layouts: 5.68 us -> none
where the time goes in v2:
time: 96.8 us; the launch traced here: 96.6 us
  Pallas kernels  96 us (99%)
    pallas_call x1, Pallas kernels, per_device(): pl.pallas_call(moe_kernel, out_shape=shapes, in_specs=[hbm, hbm, vmem, vm...  93.6 us
    pallas_call x1, Pallas kernels, per_device(): pl.pallas_call(copy_kernel, out_shape=shapes, in_specs=[vmem] * 5, out_sp...  2.36 us

profile of v2, /device:TPU:1, one launch (start us, length us, event | category | flops | bytes accessed | tf_op | source)
XLA Modules:
  0.0 96.6 jit_solution(1677770994630222986)
XLA Ops:
  0.6 93.6 %moe.1 = (bf16[128,2048]{1,0:T(8,128)(2,1)}, bf16[128,2048]{1,0:T(8,128)(2,1)}, f32[64,384]{1,0:T(8,128)}, f32[64,384]{1,0:T(8,128)}, f32[12,1,2048]{2,1,0:T(1,128)}) custom-call(bf16[128,2048]{1,0:T(8,128)(2,1)} %tok.1, bf16[128,2048]{1,0:T(8,128)(2,1)} %cot.1, s32[4,128]{1,0:T(4,128)} %bitcast.14, bf16[4,128]{1,0:T(4,128)(2,1)} %bitcast.15, ...), custom_call_target="tpu_custom_call" | custom-call | flops 14495514624 | bytes 33554432 | tf_op jit(solution)/shard_map/moe/pallas_call | solution.py:458
  94.3 2.4 %hand_out.1 = (bf16[128,2048]{1,0:T(8,128)(2,1)}, bf16[128,2048]{1,0:T(8,128)(2,1)}, f32[64,384]{1,0:T(8,128)}, f32[64,384]{1,0:T(8,128)}, f32[12,1,2048]{2,1,0:T(1,128)}) custom-call(bf16[128,2048]{1,0:T(8,128)(2,1)} %get-tuple-element.15.refs_0_, bf16[128,2048]{1,0:T(8,128)(2,1)} %get-tuple-element.16.refs_1_, f32[64,384]{1,0:T(8,128)} %get-tuple-element.17.refs_2_, ...), custom_call_target="tpu_custom_call" | custom-call | tf_op jit(solution)/shard_map/hand_out/pallas_call | solution.py:503

commit v3 on v2

--- a/solution.py
+++ b/solution.py
@@ -13,7 +13,7 @@
 NN = (((1,), (0,)), ((), ()))
 NT = (((1,), (1,)), ((), ()))
 TN = (((0,), (0,)), ((), ()))
-COPIES = 96
+COPIES = 112
 
 
 def dot(a, b, dims=NN):
@@ -44,13 +44,13 @@
 def moe_kernel(
     tok, cot, ids_t, gates_t, wg, wu, wd,
     mixed, gtok, ggate, gup, gdown,
-    X, C, G, OG, Wgu, Wd, O, SB, RY, PG, ACT, GC, APT, PT, GACC, DACC,
+    X, C, G, GT, OG, Wgu, Wd, O, SB, RY, PG, ACT, GC, APT, PT, GACC, DACC,
     S1, S2, S3, S3x, R1, R1h, R1z, R2h, R2z, R2x, R3h, R3z, R3x,
     load_sem, send_sem, recv_sem,
 ):
     T, D = tok.shape
     H = wg.shape[1]
-    CX = S1.shape[3]
+    CX = 2 * S1.shape[4]
     per = H // (NX * NZ)
     dp = lax.axis_index("dp")
     ex = lax.axis_index("expert")
@@ -86,17 +86,26 @@
         for n in names:
             desc(n).wait_recv()
 
-    for nm, buf in (("X", X), ("C", C), ("G", G)):
-        reg(nm + "s0", buf.at[0, 0], buf.at[0, 1], sib)
-        reg(nm + "p", buf.at[0, 0], buf.at[1, 0], yp)
-        reg(nm + "m", buf.at[0, 0], buf.at[2, 0], ym)
-        for i in (1, 2, 3):
-            reg(nm + "s%d" % i, buf.at[i, 0], buf.at[i, 1], sib)
-    reg("Xf", X.at[1, 0], X.at[3, 0], yp)
+    HT = T // 2
+    for nm, buf in (("X", X), ("C", C)):
+        for i in range(4):
+            reg(nm + "s%d" % i, buf.at[i, :, 0], buf.at[i, :, 1], sib)
+        for h in (0, 1):
+            reg(nm + "p%d" % h, buf.at[0, h, 0], buf.at[1 + h, 0, 0], yp)
+            reg(nm + "m%d" % h, buf.at[0, h, 0], buf.at[1 + h, 1, 0], ym)
+        reg(nm + "f0", buf.at[1, 0, 0], buf.at[3, 0, 0], yp)
+        reg(nm + "f1", buf.at[2, 1, 0], buf.at[3, 1, 0], ym)
+    for i in range(4):
+        reg("Gs%d" % i, G.at[i, 0], G.at[i, 1], sib)
+    reg("Gp", G.at[0, 0], G.at[1, 0], yp)
+    reg("Gm", G.at[0, 0], G.at[2, 0], ym)
     reg("Gf", G.at[1, 0], G.at[3, 0], yp)
-    reg("Cf", C.at[2, 0], C.at[3, 0], ym)
-    for i in range(4):
+    for i in (0, 3):
         reg("O%d" % i, O.at[i, 1], SB.at[i], sib)
+    for i in (1, 2):
+        for h in (0, 1):
+            piece = pl.ds(h * HT, HT)
+            reg("O%d%d" % (i, h), O.at[i, 1, :, piece], SB.at[i, :, piece], sib)
 
     def ring4(tag, a, b, r, plus, minus):
         reg(tag + "0", a(2), r(0), plus)
@@ -143,7 +152,6 @@
         return hop
 
     slot_of = {0: 0, -1: 1, 1: 2, 2: 3}
-    HT = T // 2
     y_mid = []
     for p in (0, 1):
         piece = pl.ds(p * HT, HT)
@@ -156,19 +164,31 @@
         ))
 
     hz = NZ // 2
-    a1 = lambda k: S1.at[at_x(k), pl.ds(0, hz)]
-    b1 = lambda k: S1.at[at_x(k), pl.ds(hz, hz)]
-    r1 = lambda i: R1.at[i]
-    s1_mid = ring4("s1x", a1, b1, r1, xp, xm)
-    rows = S1.shape[2]
+    rows = S1.shape[3]
     hr = rows // 2
-    f1z = lambda k: S1.at[x, at_z(k)]
-    s1_hop = ring8(
-        "s1z",
-        lambda k: S1.at[x, at_z(k), pl.ds(0, hr)],
-        lambda k: S1.at[x, at_z(k), pl.ds(hr, hr)],
-        f1z, lambda i: R1h.at[i], lambda i: R1z.at[i], zp, zm,
-    )
+    s1_mid, s1_hop = [], []
+    for c, tag in ((0, "s1a"), (1, "s1b")):
+        s1_mid.append(ring4(
+            tag + "x",
+            lambda k, c=c: S1.at[c, at_x(k), pl.ds(0, hz)],
+            lambda k, c=c: S1.at[c, at_x(k), pl.ds(hz, hz)],
+            lambda i, c=c: R1.at[c, i], xp, xm,
+        ))
+        s1_hop.append(ring8(
+            tag + "z",
+            lambda k, c=c: S1.at[c, x, at_z(k), pl.ds(0, hr)],
+            lambda k, c=c: S1.at[c, x, at_z(k), pl.ds(hr, hr)],
+            lambda k, c=c: S1.at[c, x, at_z(k)],
+            lambda i, c=c: R1h.at[c, i], lambda i, c=c: R1z.at[c, i], zp, zm,
+        ))
+
+    def s1_turn(c):
+        tag = ("s1a", "s1b")[c]
+        recv(tag + "x3", tag + "x4")
+        add_rows(S1.at[c, x, pl.ds(0, hz)], [R1.at[c, 3], R1.at[c, 4]])
+        recv(tag + "x2", tag + "x5")
+        add_rows(S1.at[c, x, pl.ds(hz, hz)], [R1.at[c, 2], R1.at[c, 5]])
+        start(tag + "z0", tag + "z1")
 
     hx = NX // 2
     f2 = lambda k: S2.at[at_z(k)]
@@ -196,11 +216,13 @@
     assert len(copies) <= COPIES
 
     loads = [
-        pltpu.make_async_copy(tok, X.at[0, 0], load_sem.at[0]),
-        pltpu.make_async_copy(cot, C.at[0, 0], load_sem.at[1]),
-        pltpu.make_async_copy(wg, Wgu.at[:, pl.ds(0, H)], load_sem.at[2]),
-        pltpu.make_async_copy(wu, Wgu.at[:, pl.ds(H, H)], load_sem.at[3]),
-        pltpu.make_async_copy(wd, Wd, load_sem.at[4]),
+        pltpu.make_async_copy(tok.at[pl.ds(0, HT)], X.at[0, 0, 0], load_sem.at[0]),
+        pltpu.make_async_copy(cot.at[pl.ds(0, HT)], C.at[0, 0, 0], load_sem.at[1]),
+        pltpu.make_async_copy(tok.at[pl.ds(HT, HT)], X.at[0, 1, 0], load_sem.at[2]),
+        pltpu.make_async_copy(cot.at[pl.ds(HT, HT)], C.at[0, 1, 0], load_sem.at[3]),
+        pltpu.make_async_copy(wg, Wgu.at[:, pl.ds(0, H)], load_sem.at[4]),
+        pltpu.make_async_copy(wu, Wgu.at[:, pl.ds(H, H)], load_sem.at[5]),
+        pltpu.make_async_copy(wd, Wd, load_sem.at[6]),
     ]
     for cp in loads:
         cp.start()
@@ -216,17 +238,17 @@
         dense = dense + jnp.where(ids_t[k : k + 1, :] == rows16, gates_t[k : k + 1, :].astype(F32), 0.0)
     G[0, 0] = dense.astype(BF16)
 
-    loads[0].wait()
-    loads[1].wait()
+    for cp in loads[:4]:
+        cp.wait()
     pl.semaphore_wait(barrier, len(near))
-    start("Xp", "Cm", "Gp", "Gm", "Gs0", "Xs0", "Cs0", "Cp", "Xm")
+    start("Gp", "Gm", "Xp0", "Xm0", "Cp0", "Cm0", "Xp1", "Xm1", "Cp1", "Cm1", "Gs0", "Xs0", "Cs0")
 
     q = lax.broadcasted_iota(jnp.int32, PT.shape, 0)
     unit = lax.broadcasted_iota(jnp.int32, PT.shape, 1)
     row = ((unit // per) % NZ) * (NX * per) + (unit // (per * NZ)) * per + unit % per
     PT[...] = jnp.where(q == row, 1.0, 0.0).astype(BF16)
 
-    for cp in loads[2:]:
+    for cp in loads[4:]:
         cp.wait()
 
     mine = (rows16 == ex).astype(F32).astype(BF16)
@@ -234,10 +256,18 @@
     def rows_of(i):
         return pl.ds(pl.multiple_of(i * 2 * T, 2 * T), 2 * T)
 
+    def place(i, p):
+        own = (i == 0) | (i == 3)
+        return jnp.where(own, i, 1 + p), jnp.where(own, p, i - 1)
+
     def hidden(i):
-        gate = jnp.concatenate([dot(G[i, s], mine, TN) for s in (0, 1)], axis=0)
-        GC[...] = gate
-        gate = gate[:, :1]
+        for p in (0, 1):
+            slot, half = place(i, p)
+            for s in (0, 1):
+                GT[p, s] = dot(G[slot, s], mine, TN)
+                at = (p * 2 + s) * HT
+                GC[at : at + HT, :] = GT[p, s, pl.ds(pl.multiple_of(half * HT, HT), HT), :]
+        gate = GC[:, :1]
         here = rows_of(i)
         inputs = X[i].reshape(2 * T, D)
         out_grad = (C[i].reshape(2 * T, D).astype(F32) * gate).astype(BF16)
@@ -259,14 +289,18 @@
             cols = pl.ds(pl.multiple_of(n * 512, 512), 512)
             part = (dot(ACT[...], Wd[:, cols]) * GC[:, :1]).astype(BF16)
             grad = dot(PG[rows_of(i), :], Wgu[cols, :], NT).astype(BF16)
-            for s in (0, 1):
-                O[i, s, 0, :, cols] = part[s * T : (s + 1) * T]
-                O[i, s, 1, :, cols] = grad[s * T : (s + 1) * T]
+            for p in (0, 1):
+                slot, half = place(i, p)
+                to = pl.ds(pl.multiple_of(half * HT, HT), HT)
+                for s in (0, 1):
+                    at = (p * 2 + s) * HT
+                    O[slot, s, 0, to, cols] = part[at : at + HT]
+                    O[slot, s, 1, to, cols] = grad[at : at + HT]
 
     def gate_up_part(m, first, count):
         cols = pl.ds(pl.multiple_of(m * 256, 256), 256)
         span = pl.ds(first * 2 * T, count * 2 * T)
-        return dot(X[pl.ds(first, count), :, :, cols].reshape(count * 2 * T, 256), PG[span, :], TN)
+        return dot(X[pl.ds(first, count), :, :, :, cols].reshape(count * 2 * T, 256), PG[span, :], TN)
 
     def down_part(n, first, count):
         cols = pl.ds(pl.multiple_of(n * 512, 512), 512)
@@ -302,12 +336,13 @@
             m = xx * 2 + half
             here = pl.ds(pl.multiple_of(m * 256, 256), 256)
             new = (GACC[here, :] + gate_up_part(m, 3, 1)).astype(BF16)
-            S1[xx, pl.ds(half * hz, hz)] = new[:, :CX].reshape(hz, rows, CX)
+            for c in (0, 1):
+                S1[c, xx, pl.ds(half * hz, hz)] = new[:, c * (CX // 2) : (c + 1) * (CX // 2)].reshape(hz, rows, CX // 2)
             S2[pl.ds(half * hz, hz), xx] = new[:, CX:].reshape(hz, rows, 2 * H - CX)
-            for at, name in ((0, "s1x0"), (1, "s1x1"), (3, "s1x2"), (4, "s1x3")):
+            for at, name in ((0, "x0"), (1, "x1"), (3, "x2"), (4, "x3")):
                 @pl.when(t == at)
                 def _():
-                    start(name)
+                    start("s1a" + name, "s1b" + name)
 
         start("s2z0", "s2z1")
 
@@ -316,6 +351,14 @@
         for a in (0, 1):
             add_rows(O.at[i, 0, a], [SB.at[i, a]])
 
+    def fold_half(h):
+        piece = pl.ds(h * HT, HT)
+        for i in (1, 2):
+            recv("O%d%d" % (i, h))
+            for a in (0, 1):
+                add_rows(O.at[i, 0, a, piece], [SB.at[i, a, piece]])
+        start("y%d3" % h, "y%d2" % h)
+
     def step(i, carry):
         @pl.when(i == 0)
         def _():
@@ -324,26 +367,34 @@
         @pl.when(i == 1)
         def _():
             partial(0, 1, True)
-            recv("Xp", "Cm", "Gp", "Gm")
-            start("Xf", "Cf", "Gf", "Gs1", "Gs2", "Xs1", "Cs2")
-            recv("Cp", "Xm")
-            start("Cs1", "Xs2")
-            recv("Xs1", "Cs1", "Gs1")
+            recv("Gp", "Gm")
+            start("Gs1", "Gs2", "Gf")
+            recv("Xp0", "Cp0")
+            start("Xf0", "Cf0")
+            recv("Xm0", "Cm0")
+            start("Xs1", "Cs1")
+            recv("Gs1", "Gs2", "Xs1", "Cs1")
 
         @pl.when(i == 2)
         def _():
-            recv("Xs2", "Cs2", "Gs2")
+            partial(1, 1, False)
+            recv("Gf")
+            start("Gs3")
+            recv("Xm1", "Cm1")
+            start("Xf1", "Cf1")
+            recv("Xp1", "Cp1")
+            start("Xs2", "Cs2")
+            fold_half(0)
+            recv("Xs2", "Cs2")
 
         @pl.when(i == 3)
         def _():
-            fold(1)
-            start("y03", "y13")
-            fold(2)
-            start("y02", "y12")
-            recv("Xf", "Cf", "Gf")
-            start("Gs3", "Xs3", "Cs3")
-            partial(1, 2, False)
-            recv("Xs3", "Cs3", "Gs3")
+            partial(2, 1, False)
+            fold_half(1)
+            fold(0)
+            recv("Xf0", "Cf0", "Xf1", "Cf1")
+            start("Xs3", "Cs3")
+            recv("Gs3", "Xs3", "Cs3")
 
         hidden(i)
 
@@ -352,10 +403,10 @@
             finish()
 
         outputs(i)
-        for k in range(4):
+        for k, names in ((0, ("O0",)), (1, ("O10", "O20")), (2, ("O11", "O21")), (3, ("O3",))):
             @pl.when(i == k)
             def _():
-                start("O%d" % k)
+                start(*names)
         return carry
 
     lax.fori_loop(0, 4, step, 0)
@@ -373,59 +424,78 @@
                 O[0, 0, 1, sl, :].astype(F32) + RY[2, sl, :].astype(F32) + RY[5, sl, :].astype(F32)
             ).astype(BF16)
 
+    def s3_turn():
+        recv("s3zp1", "s3zm1")
+        p_row = lax.broadcasted_iota(jnp.int32, (NX * 16, NX * per), 0)
+        p_unit = lax.broadcasted_iota(jnp.int32, (NX * 16, NX * per), 1)
+        apart = jnp.where(p_row == (p_unit // per) * 16 + p_unit % per, 1.0, 0.0).astype(BF16)
+
+        @pl.loop(0, D // 512)
+        def _(n):
+            cols = pl.ds(pl.multiple_of(n * 512, 512), 512)
+            total = S3[z, :, cols].astype(F32) + R3z[4, :, cols].astype(F32) + R3z[5, :, cols].astype(F32)
+            S3x[:, :, cols] = dot(apart, total.astype(BF16)).astype(BF16).reshape(NX, 16, 512)
+
+        start("s3x0", "s3x1", "s3x2", "s3x3")
+
+    def s2_turn():
+        recv("s2zp1", "s2zm1")
+        add_rows(f2(0), [R2z.at[4], R2z.at[5]])
+        start("s2x0", "s2x1", "s2x2", "s2x3")
+
+    def s3_end():
+        recv("s3x2", "s3x3", "s3x4", "s3x5")
+        low = a3(0)[...].astype(F32) + R3x[3].astype(F32) + R3x[4].astype(F32)
+        high = b3(0)[...].astype(F32) + R3x[2].astype(F32) + R3x[5].astype(F32)
+        for j in range(per):
+            gdown[j, :, :hd] = low[j : j + 1]
+            gdown[j, :, hd:] = high[j : j + 1]
+
+    def s2_end():
+        recv("s2x2", "s2x3", "s2x4", "s2x5")
+        gup[:hr, CX - H :] = a2(0)[...].astype(F32) + R2x[3].astype(F32) + R2x[4].astype(F32)
+        gup[hr:, CX - H :] = b2(0)[...].astype(F32) + R2x[2].astype(F32) + R2x[5].astype(F32)
+
+    def s1_end(c):
+        tag = ("s1a", "s1b")[c]
+        recv(tag + "zp1", tag + "zm1")
+        total = S1[c, x, z].astype(F32) + R1z[c, 4].astype(F32) + R1z[c, 5].astype(F32)
+        if c == 0:
+            ggate[:, : CX // 2] = total
+        else:
+            ggate[:, CX // 2 :] = total[:, : H - CX // 2]
+            gup[:, : CX - H] = total[:, H - CX // 2 :]
+
     s3_hop(3)
+    s2_hop(3)
     fold(3)
     start("y00", "y01", "y10", "y11")
-    s2_hop(3)
-    s1_mid()
-    fold(0)
+    s1_mid[0]()
+    s1_mid[1]()
     s3_hop(2)
     s2_hop(2)
+    s1_turn(0)
+    s3_hop(1)
+    s1_turn(1)
     y_mid[0]()
-    s3_hop(1)
-    recv("s1x3", "s1x4")
-    add_rows(a1(0), [r1(3), r1(4)])
-    recv("s1x2", "s1x5")
-    add_rows(b1(0), [r1(2), r1(5)])
-    start("s1z0", "s1z1")
+    s2_hop(1)
     y_mid[1]()
-    s2_hop(1)
-    s1_hop(3)
-
-    recv("s3zp1", "s3zm1")
-    p_row = lax.broadcasted_iota(jnp.int32, (NX * 16, NX * per), 0)
-    p_unit = lax.broadcasted_iota(jnp.int32, (NX * 16, NX * per), 1)
-    apart = jnp.where(p_row == (p_unit // per) * 16 + p_unit % per, 1.0, 0.0).astype(BF16)
-
-    @pl.loop(0, D // 512)
-    def _(n):
-        cols = pl.ds(pl.multiple_of(n * 512, 512), 512)
-        total = S3[z, :, cols].astype(F32) + R3z[4, :, cols].astype(F32) + R3z[5, :, cols].astype(F32)
-        S3x[:, :, cols] = dot(apart, total.astype(BF16)).astype(BF16).reshape(NX, 16, 512)
-
-    start("s3x0", "s3x1", "s3x2", "s3x3")
-    s1_hop(2)
-    recv("s2zp1", "s2zm1")
-    add_rows(f2(0), [R2z.at[4], R2z.at[5]])
-    start("s2x0", "s2x1", "s2x2", "s2x3")
+    s1_hop[0](3)
+    s3_turn()
+    s1_hop[1](3)
+    s2_turn()
+    s1_hop[0](2)
     s3_mid()
+    s1_hop[1](2)
     y_final(0)
-    s1_hop(1)
     s2_mid()
-    recv("s3x2", "s3x3", "s3x4", "s3x5")
-    low = a3(0)[...].astype(F32) + R3x[3].astype(F32) + R3x[4].astype(F32)
-    high = b3(0)[...].astype(F32) + R3x[2].astype(F32) + R3x[5].astype(F32)
-    for j in range(per):
-        gdown[j, :, :hd] = low[j : j + 1]
-        gdown[j, :, hd:] = high[j : j + 1]
+    s1_hop[0](1)
+    s3_end()
+    s1_hop[1](1)
+    s2_end()
     y_final(1)
-    recv("s2x2", "s2x3", "s2x4", "s2x5")
-    gup[:hr, CX - H :] = a2(0)[...].astype(F32) + R2x[3].astype(F32) + R2x[4].astype(F32)
-    gup[hr:, CX - H :] = b2(0)[...].astype(F32) + R2x[2].astype(F32) + R2x[5].astype(F32)
-    recv("s1zp1", "s1zm1")
-    total = f1z(0)[...].astype(F32) + R1z[4].astype(F32) + R1z[5].astype(F32)
-    ggate[...] = total[:, :H]
-    gup[:, : CX - H] = total[:, H:]
+    s1_end(0)
+    s1_end(1)
 
     for n in copies:
         desc(n).wait_send()
@@ -461,9 +531,10 @@
         in_specs=[hbm, hbm, vmem, vmem, hbm, hbm, hbm],
         out_specs=(vmem,) * 5,
         scratch_shapes=[
-            V((4, 2, T, D), BF16),
-            V((4, 2, T, D), BF16),
+            V((4, 2, 2, T // 2, D), BF16),
+            V((4, 2, 2, T // 2, D), BF16),
             V((4, 2, 16, T), BF16),
+            V((2, 2, T, 128), F32),
             V((8 * T, D), BF16),
             V((D, 2 * H), BF16),
             V((H, D), BF16),
@@ -477,20 +548,20 @@
             V((H, H), BF16),
             V((D, 2 * H), F32),
             V((H, D), F32),
-            V((NX, NZ, rows, CX), BF16),
+            V((2, NX, NZ, rows, CX // 2), BF16),
             V((NZ, NX, rows, CZ), BF16),
             V((NZ, NX * per, D), BF16),
             V((NX, 16, D), BF16),
-            V((6, NZ // 2, rows, CX), BF16),
-            V((2, rows // 2, CX), BF16),
-            V((6, rows, CX), BF16),
+            V((2, 6, NZ // 2, rows, CX // 2), BF16),
+            V((2, 2, rows // 2, CX // 2), BF16),
+            V((2, 6, rows, CX // 2), BF16),
             V((2, NX // 2, rows, CZ), BF16),
             V((6, NX, rows, CZ), BF16),
             V((6, rows // 2, CZ), BF16),
             V((2, NX * per, D // 2), BF16),
             V((6, NX * per, D), BF16),
             V((6, 16, D // 2), BF16),
-            pltpu.SemaphoreType.DMA((5,)),
+            pltpu.SemaphoreType.DMA((7,)),
             pltpu.SemaphoreType.DMA((COPIES,)),
             pltpu.SemaphoreType.DMA((COPIES,)),
         ],

time: 96.8 us -> 96.1 us (level)
  no operation moved by 1% of the time
where the time goes in v3:
time: 96.1 us; the launch traced here: 96 us
  Pallas kernels  95.4 us (99%)
    pallas_call x1, Pallas kernels, per_device(): pl.pallas_call(moe_kernel, out_shape=shapes, in_specs=[hbm, hbm, vmem, vm...  93 us
    pallas_call x1, Pallas kernels, per_device(): pl.pallas_call(copy_kernel, out_shape=shapes, in_specs=[vmem] * 5, out_sp...  2.36 us

profile of v3, /device:TPU:1, one launch (start us, length us, event | category | flops | bytes accessed | tf_op | source)
XLA Modules:
  0.0 96.0 jit_solution(9073502172388888235)
XLA Ops:
  0.6 93.0 %moe.1 = (bf16[128,2048]{1,0:T(8,128)(2,1)}, bf16[128,2048]{1,0:T(8,128)(2,1)}, f32[64,384]{1,0:T(8,128)}, f32[64,384]{1,0:T(8,128)}, f32[12,1,2048]{2,1,0:T(1,128)}) custom-call(bf16[128,2048]{1,0:T(8,128)(2,1)} %tok.1, bf16[128,2048]{1,0:T(8,128)(2,1)} %cot.1, s32[4,128]{1,0:T(4,128)} %bitcast.14, bf16[4,128]{1,0:T(4,128)(2,1)} %bitcast.15, ...), custom_call_target="tpu_custom_call" | custom-call | flops 14495514624 | bytes 33554432 | tf_op jit(solution)/shard_map/moe/pallas_call | solution.py:528
  93.7 2.4 %hand_out.1 = (bf16[128,2048]{1,0:T(8,128)(2,1)}, bf16[128,2048]{1,0:T(8,128)(2,1)}, f32[64,384]{1,0:T(8,128)}, f32[64,384]{1,0:T(8,128)}, f32[12,1,2048]{2,1,0:T(1,128)}) custom-call(bf16[128,2048]{1,0:T(8,128)(2,1)} %get-tuple-element.15.refs_0_, bf16[128,2048]{1,0:T(8,128)(2,1)} %get-tuple-element.16.refs_1_, f32[64,384]{1,0:T(8,128)} %get-tuple-element.17.refs_2_, ...), custom_call_target="tpu_custom_call" | custom-call | tf_op jit(solution)/shard_map/hand_out/pallas_call | solution.py:574

commit v4 on v3

--- a/solution.py
+++ b/solution.py
@@ -44,7 +44,7 @@
 def moe_kernel(
     tok, cot, ids_t, gates_t, wg, wu, wd,
     mixed, gtok, ggate, gup, gdown,
-    X, C, G, GT, OG, Wgu, Wd, O, SB, RY, PG, ACT, GC, APT, PT, GACC, DACC,
+    X, C, G, GT, OG, Wgu, Wd, O, SB, RY, PG, ACT, SILU, SLOPE, GC, APT, PT, GACC, DACC,
     S1, S2, S3, S3x, R1, R1h, R1z, R2h, R2z, R2x, R3h, R3z, R3x,
     load_sem, send_sem, recv_sem,
 ):
@@ -88,8 +88,10 @@
 
     HT = T // 2
     for nm, buf in (("X", X), ("C", C)):
-        for i in range(4):
+        for i in range(3):
             reg(nm + "s%d" % i, buf.at[i, :, 0], buf.at[i, :, 1], sib)
+        for h in (0, 1):
+            reg(nm + "s3%d" % h, buf.at[3, h, 0], buf.at[3, h, 1], sib)
         for h in (0, 1):
             reg(nm + "p%d" % h, buf.at[0, h, 0], buf.at[1 + h, 0, 0], yp)
             reg(nm + "m%d" % h, buf.at[0, h, 0], buf.at[1 + h, 1, 0], ym)
@@ -100,8 +102,9 @@
     reg("Gp", G.at[0, 0], G.at[1, 0], yp)
     reg("Gm", G.at[0, 0], G.at[2, 0], ym)
     reg("Gf", G.at[1, 0], G.at[3, 0], yp)
-    for i in (0, 3):
-        reg("O%d" % i, O.at[i, 1], SB.at[i], sib)
+    reg("O0", O.at[0, 1], SB.at[0], sib)
+    for a in (0, 1):
+        reg("O3%d" % a, O.at[3, 1, a], SB.at[3, a], sib)
     for i in (1, 2):
         for h in (0, 1):
             piece = pl.ds(h * HT, HT)
@@ -215,6 +218,11 @@
     s3_mid = ring4("s3x", a3, b3, lambda i: R3x.at[i], xp, xm)
     assert len(copies) <= COPIES
 
+    barrier = pltpu.get_barrier_semaphore()
+    near = (sib, yp, ym, xp, xm, zp, zm)
+    for dev in near:
+        pl.semaphore_signal(barrier, inc=1, device_id=dev, device_id_type=pl.DeviceIdType.MESH)
+
     loads = [
         pltpu.make_async_copy(tok.at[pl.ds(0, HT)], X.at[0, 0, 0], load_sem.at[0]),
         pltpu.make_async_copy(cot.at[pl.ds(0, HT)], C.at[0, 0, 0], load_sem.at[1]),
@@ -227,11 +235,6 @@
     for cp in loads:
         cp.start()
 
-    barrier = pltpu.get_barrier_semaphore()
-    near = (sib, yp, ym, xp, xm, zp, zm)
-    for dev in near:
-        pl.semaphore_signal(barrier, inc=1, device_id=dev, device_id_type=pl.DeviceIdType.MESH)
-
     rows16 = lax.broadcasted_iota(jnp.int32, (16, T), 0)
     dense = jnp.zeros((16, T), F32)
     for k in range(ids_t.shape[0]):
@@ -260,96 +263,105 @@
         own = (i == 0) | (i == 3)
         return jnp.where(own, i, 1 + p), jnp.where(own, p, i - 1)
 
-    def hidden(i):
+    def from_tokens(i):
         for p in (0, 1):
             slot, half = place(i, p)
             for s in (0, 1):
                 GT[p, s] = dot(G[slot, s], mine, TN)
                 at = (p * 2 + s) * HT
                 GC[at : at + HT, :] = GT[p, s, pl.ds(pl.multiple_of(half * HT, HT), HT), :]
-        gate = GC[:, :1]
-        here = rows_of(i)
-        inputs = X[i].reshape(2 * T, D)
-        out_grad = (C[i].reshape(2 * T, D).astype(F32) * gate).astype(BF16)
-        OG[here, :] = out_grad
-        pre = dot(inputs, Wgu[...])
-        act_grad = dot(out_grad, Wd[...], NT)
+        pre = dot(X[i].reshape(2 * T, D), Wgu[...])
         pre_gate, pre_up = pre[:, :H], pre[:, H:]
         sig = 1.0 / (1.0 + jnp.exp(-pre_gate))
         silu = pre_gate * sig
         activated = (silu * pre_up).astype(BF16)
         ACT[...] = activated
-        PG[here, H:] = (act_grad * silu).astype(BF16)
-        PG[here, :H] = (act_grad * pre_up * sig * (1.0 + pre_gate * (1.0 - sig))).astype(BF16)
-        APT[:, here] = dot(PT[...], activated, NT).astype(BF16)
-
-    def outputs(i):
-        @pl.loop(0, D // 512)
+        SILU[...] = silu
+        SLOPE[...] = pre_up * sig * (1.0 + pre_gate * (1.0 - sig))
+        APT[:, rows_of(i)] = dot(PT[...], activated, NT).astype(BF16)
+        store(i, 0, lambda cols: dot(ACT[...], Wd[:, cols]) * GC[:, :1])
+
+    def from_cotangents(i):
+        here = rows_of(i)
+        out_grad = (C[i].reshape(2 * T, D).astype(F32) * GC[:, :1]).astype(BF16)
+        OG[here, :] = out_grad
+        act_grad = dot(out_grad, Wd[...], NT)
+        PG[here, H:] = (act_grad * SILU[...]).astype(BF16)
+        PG[here, :H] = (act_grad * SLOPE[...]).astype(BF16)
+
+    def token_grads(i):
+        store(i, 1, lambda cols: dot(PG[rows_of(i), :], Wgu[cols, :], NT))
+
+    def store(i, a, value):
+        @pl.loop(0, D // 1024)
         def _(n):
-            cols = pl.ds(pl.multiple_of(n * 512, 512), 512)
-            part = (dot(ACT[...], Wd[:, cols]) * GC[:, :1]).astype(BF16)
-            grad = dot(PG[rows_of(i), :], Wgu[cols, :], NT).astype(BF16)
+            cols = pl.ds(pl.multiple_of(n * 1024, 1024), 1024)
+            result = value(cols).astype(BF16)
             for p in (0, 1):
                 slot, half = place(i, p)
                 to = pl.ds(pl.multiple_of(half * HT, HT), HT)
                 for s in (0, 1):
                     at = (p * 2 + s) * HT
-                    O[slot, s, 0, to, cols] = part[at : at + HT]
-                    O[slot, s, 1, to, cols] = grad[at : at + HT]
+                    O[slot, s, a, to, cols] = result[at : at + HT]
+
+    TILE = D // NX
 
     def gate_up_part(m, first, count):
-        cols = pl.ds(pl.multiple_of(m * 256, 256), 256)
+        cols = pl.ds(pl.multiple_of(m * TILE, TILE), TILE)
         span = pl.ds(first * 2 * T, count * 2 * T)
-        return dot(X[pl.ds(first, count), :, :, :, cols].reshape(count * 2 * T, 256), PG[span, :], TN)
+        return dot(X[pl.ds(first, count), :, :, :, cols].reshape(count * 2 * T, TILE), PG[span, :], TN)
 
     def down_part(n, first, count):
-        cols = pl.ds(pl.multiple_of(n * 512, 512), 512)
+        cols = pl.ds(pl.multiple_of(n * 1024, 1024), 1024)
         span = pl.ds(first * 2 * T, count * 2 * T)
         return dot(APT[:, span], OG[span, cols])
 
     def partial(first, count, fresh):
-        @pl.loop(0, D // 256)
+        @pl.loop(0, NX)
         def _(m):
-            here = pl.ds(pl.multiple_of(m * 256, 256), 256)
+            here = pl.ds(pl.multiple_of(m * TILE, TILE), TILE)
             new = gate_up_part(m, first, count)
             GACC[here, :] = new if fresh else GACC[here, :] + new
 
-        @pl.loop(0, D // 512)
+        @pl.loop(0, D // 1024)
         def _(n):
-            cols = pl.ds(pl.multiple_of(n * 512, 512), 512)
+            cols = pl.ds(pl.multiple_of(n * 1024, 1024), 1024)
             new = down_part(n, first, count)
             DACC[:, cols] = new if fresh else DACC[:, cols] + new
 
     def finish():
-        @pl.loop(0, D // 512)
+        @pl.loop(0, D // 1024)
         def _(n):
-            cols = pl.ds(pl.multiple_of(n * 512, 512), 512)
-            S3[:, :, cols] = (DACC[:, cols] + down_part(n, 3, 1)).astype(BF16).reshape(NZ, NX * per, 512)
+            cols = pl.ds(pl.multiple_of(n * 1024, 1024), 1024)
+            S3[:, :, cols] = (DACC[:, cols] + down_part(n, 3, 1)).astype(BF16).reshape(NZ, NX * per, 1024)
 
         start("s3z0", "s3z1")
 
-        @pl.loop(0, 8)
-        def _(t):
-            k = t // 2
+        @pl.loop(0, NX)
+        def _(k):
             xx = (x + jnp.where(k == 0, 2, jnp.where(k == 1, 1, jnp.where(k == 2, 3, 0)))) % NX
-            half = t % 2
-            m = xx * 2 + half
-            here = pl.ds(pl.multiple_of(m * 256, 256), 256)
-            new = (GACC[here, :] + gate_up_part(m, 3, 1)).astype(BF16)
+            here = pl.ds(pl.multiple_of(xx * TILE, TILE), TILE)
+            new = (GACC[here, :] + gate_up_part(xx, 3, 1)).astype(BF16)
             for c in (0, 1):
-                S1[c, xx, pl.ds(half * hz, hz)] = new[:, c * (CX // 2) : (c + 1) * (CX // 2)].reshape(hz, rows, CX // 2)
-            S2[pl.ds(half * hz, hz), xx] = new[:, CX:].reshape(hz, rows, 2 * H - CX)
-            for at, name in ((0, "x0"), (1, "x1"), (3, "x2"), (4, "x3")):
-                @pl.when(t == at)
+                S1[c, xx] = new[:, c * (CX // 2) : (c + 1) * (CX // 2)].reshape(NZ, rows, CX // 2)
+            S2[:, xx] = new[:, CX:].reshape(NZ, rows, 2 * H - CX)
+            for at, names in ((0, ("x0", "x1")), (1, ("x2",)), (2, ("x3",))):
+                @pl.when(k == at)
                 def _():
-                    start("s1a" + name, "s1b" + name)
+                    for name in names:
+                        start("s1a" + name, "s1b" + name)
 
         start("s2z0", "s2z1")
 
-    def fold(i):
-        recv("O%d" % i)
+    def fold_own():
+        recv("O0")
         for a in (0, 1):
-            add_rows(O.at[i, 0, a], [SB.at[i, a]])
+            add_rows(O.at[0, 0, a], [SB.at[0, a]])
+
+    def fold_far(a):
+        recv("O3%d" % a)
+        add_rows(O.at[3, 0, a], [SB.at[3, a]])
+        start("y0%d" % a, "y1%d" % a)
 
     def fold_half(h):
         piece = pl.ds(h * HT, HT)
@@ -389,21 +401,35 @@
 
         @pl.when(i == 3)
         def _():
+            recv("Xf0")
+            start("Xs30")
+            recv("Xf1")
+            start("Xs31")
             partial(2, 1, False)
+            recv("Gs3", "Xs30", "Xs31")
+
+        from_tokens(i)
+
+        @pl.when(i == 3)
+        def _():
+            start("O30")
+            recv("Cf0")
+            start("Cs30")
+            recv("Cf1")
+            start("Cs31")
             fold_half(1)
-            fold(0)
-            recv("Xf0", "Cf0", "Xf1", "Cf1")
-            start("Xs3", "Cs3")
-            recv("Gs3", "Xs3", "Cs3")
-
-        hidden(i)
+            recv("Cs30", "Cs31")
+
+        from_cotangents(i)
 
         @pl.when(i == 3)
         def _():
             finish()
-
-        outputs(i)
-        for k, names in ((0, ("O0",)), (1, ("O10", "O20")), (2, ("O11", "O21")), (3, ("O3",))):
+            fold_far(0)
+            fold_own()
+
+        token_grads(i)
+        for k, names in ((0, ("O0",)), (1, ("O10", "O20")), (2, ("O11", "O21")), (3, ("O31",))):
             @pl.when(i == k)
             def _():
                 start(*names)
@@ -468,32 +494,31 @@
 
     s3_hop(3)
     s2_hop(3)
-    fold(3)
-    start("y00", "y01", "y10", "y11")
+    fold_far(1)
     s1_mid[0]()
-    s1_mid[1]()
     s3_hop(2)
     s2_hop(2)
+    s1_mid[1]()
     s1_turn(0)
+    y_mid[0]()
     s3_hop(1)
     s1_turn(1)
-    y_mid[0]()
     s2_hop(1)
+    s1_hop[0](3)
     y_mid[1]()
-    s1_hop[0](3)
     s3_turn()
     s1_hop[1](3)
+    y_final(0)
     s2_turn()
     s1_hop[0](2)
     s3_mid()
     s1_hop[1](2)
-    y_final(0)
     s2_mid()
     s1_hop[0](1)
     s3_end()
     s1_hop[1](1)
+    y_final(1)
     s2_end()
-    y_final(1)
     s1_end(0)
     s1_end(1)
 
@@ -543,6 +568,8 @@
             V((6, T, D), BF16),
             V((8 * T, 2 * H), BF16),
             V((2 * T, H), BF16),
+            V((2 * T, H), F32),
+            V((2 * T, H), F32),
             V((2 * T, 128), F32),
             V((H, 8 * T), BF16),
             V((H, H), BF16),

time: 96.1 us -> 94 us (0.978)
  Pallas kernels: 95.4 us -> 93.1 us
    pallas_call x1, Pallas kernels: 93 us -> 90.8 us  [per_device(): pl.pallas_call(moe_kernel, out_shape=shapes, in_specs=[hbm, hbm, vmem, vm...]
where the time goes in v4:
time: 94 us; the launch traced here: 93.8 us
  Pallas kernels  93.1 us (99%)
    pallas_call x1, Pallas kernels, per_device(): pl.pallas_call(moe_kernel, out_shape=shapes, in_specs=[hbm, hbm, vmem, vm...  90.8 us
    pallas_call x1, Pallas kernels, per_device(): pl.pallas_call(copy_kernel, out_shape=shapes, in_specs=[vmem] * 5, out_sp...  2.36 us

profile of v4, /device:TPU:1, one launch (start us, length us, event | category | flops | bytes accessed | tf_op | source)
XLA Modules:
  0.0 93.8 jit_solution(10646767140106741104)
XLA Ops:
  0.6 90.8 %moe.1 = (bf16[128,2048]{1,0:T(8,128)(2,1)}, bf16[128,2048]{1,0:T(8,128)(2,1)}, f32[64,384]{1,0:T(8,128)}, f32[64,384]{1,0:T(8,128)}, f32[12,1,2048]{2,1,0:T(1,128)}) custom-call(bf16[128,2048]{1,0:T(8,128)(2,1)} %tok.1, bf16[128,2048]{1,0:T(8,128)(2,1)} %cot.1, s32[4,128]{1,0:T(4,128)} %bitcast.14, bf16[4,128]{1,0:T(4,128)(2,1)} %bitcast.15, ...), custom_call_target="tpu_custom_call" | custom-call | flops 14495514624 | bytes 33554432 | tf_op jit(solution)/shard_map/moe/pallas_call | solution.py:553
  91.4 2.4 %hand_out.1 = (bf16[128,2048]{1,0:T(8,128)(2,1)}, bf16[128,2048]{1,0:T(8,128)(2,1)}, f32[64,384]{1,0:T(8,128)}, f32[64,384]{1,0:T(8,128)}, f32[12,1,2048]{2,1,0:T(1,128)}) custom-call(bf16[128,2048]{1,0:T(8,128)(2,1)} %get-tuple-element.15.refs_0_, bf16[128,2048]{1,0:T(8,128)(2,1)} %get-tuple-element.16.refs_1_, f32[64,384]{1,0:T(8,128)} %get-tuple-element.17.refs_2_, ...), custom_call_target="tpu_custom_call" | custom-call | tf_op jit(solution)/shard_map/hand_out/pallas_call | solution.py:601

commit v5 on v4

--- a/solution.py
+++ b/solution.py
@@ -20,6 +20,15 @@
     return lax.dot_general(a, b, dims, preferred_element_type=F32)
 
 
+def total_of(terms):
+    if len(terms) == 2:
+        return terms[0] + terms[1]
+    total = terms[0].astype(F32)
+    for t in terms[1:]:
+        total = total + t.astype(F32)
+    return total.astype(BF16)
+
+
 def add_rows(dst, srcs):
     rows = dst.shape[-2]
     step = 16 if rows % 16 == 0 else rows
@@ -28,17 +37,11 @@
         @pl.loop(0, rows // step)
         def _(i):
             sl = pl.ds(pl.multiple_of(i * step, step), step)
-            total = dst[sl, :].astype(F32)
-            for s in srcs:
-                total = total + s[sl, :].astype(F32)
-            dst[sl, :] = total.astype(dst.dtype)
+            dst[sl, :] = total_of([dst[sl, :]] + [s[sl, :] for s in srcs])
     else:
         @pl.loop(0, dst.shape[0])
         def _(i):
-            total = dst[i].astype(F32)
-            for s in srcs:
-                total = total + s[i].astype(F32)
-            dst[i] = total.astype(dst.dtype)
+            dst[i] = total_of([dst[i]] + [s[i] for s in srcs])
 
 
 def moe_kernel(
@@ -426,7 +429,6 @@
         def _():
             finish()
             fold_far(0)
-            fold_own()
 
         token_grads(i)
         for k, names in ((0, ("O0",)), (1, ("O10", "O20")), (2, ("O11", "O21")), (3, ("O31",))):
@@ -456,11 +458,11 @@
         p_unit = lax.broadcasted_iota(jnp.int32, (NX * 16, NX * per), 1)
         apart = jnp.where(p_row == (p_unit // per) * 16 + p_unit % per, 1.0, 0.0).astype(BF16)
 
-        @pl.loop(0, D // 512)
+        @pl.loop(0, D // 1024)
         def _(n):
-            cols = pl.ds(pl.multiple_of(n * 512, 512), 512)
+            cols = pl.ds(pl.multiple_of(n * 1024, 1024), 1024)
             total = S3[z, :, cols].astype(F32) + R3z[4, :, cols].astype(F32) + R3z[5, :, cols].astype(F32)
-            S3x[:, :, cols] = dot(apart, total.astype(BF16)).astype(BF16).reshape(NX, 16, 512)
+            S3x[:, :, cols] = dot(apart, total.astype(BF16)).astype(BF16).reshape(NX, 16, 1024)
 
         start("s3x0", "s3x1", "s3x2", "s3x3")
 
@@ -495,6 +497,7 @@
     s3_hop(3)
     s2_hop(3)
     fold_far(1)
+    fold_own()
     s1_mid[0]()
     s3_hop(2)
     s2_hop(2)

time: 94 us -> 94 us (level)
  no operation moved by 1% of the time
where the time goes in v5:
time: 94 us; the launch traced here: 93.7 us
  Pallas kernels  93.1 us (99%)
    pallas_call x1, Pallas kernels, per_device(): pl.pallas_call(moe_kernel, out_shape=shapes, in_specs=[hbm, hbm, vmem, vm...  90.7 us
    pallas_call x1, Pallas kernels, per_device(): pl.pallas_call(copy_kernel, out_shape=shapes, in_specs=[vmem] * 5, out_sp...  2.36 us

profile of v5, /device:TPU:1, one launch (start us, length us, event | category | flops | bytes accessed | tf_op | source)
XLA Modules:
  0.0 93.7 jit_solution(10907677361919030408)
XLA Ops:
  0.6 90.7 %moe.1 = (bf16[128,2048]{1,0:T(8,128)(2,1)}, bf16[128,2048]{1,0:T(8,128)(2,1)}, f32[64,384]{1,0:T(8,128)}, f32[64,384]{1,0:T(8,128)}, f32[12,1,2048]{2,1,0:T(1,128)}) custom-call(bf16[128,2048]{1,0:T(8,128)(2,1)} %tok.1, bf16[128,2048]{1,0:T(8,128)(2,1)} %cot.1, s32[4,128]{1,0:T(4,128)} %bitcast.14, bf16[4,128]{1,0:T(4,128)(2,1)} %bitcast.15, ...), custom_call_target="tpu_custom_call" | custom-call | flops 14495514624 | bytes 33554432 | tf_op jit(solution)/shard_map/moe/pallas_call | solution.py:556
  91.4 2.4 %hand_out.1 = (bf16[128,2048]{1,0:T(8,128)(2,1)}, bf16[128,2048]{1,0:T(8,128)(2,1)}, f32[64,384]{1,0:T(8,128)}, f32[64,384]{1,0:T(8,128)}, f32[12,1,2048]{2,1,0:T(1,128)}) custom-call(bf16[128,2048]{1,0:T(8,128)(2,1)} %get-tuple-element.15.refs_0_, bf16[128,2048]{1,0:T(8,128)(2,1)} %get-tuple-element.16.refs_1_, f32[64,384]{1,0:T(8,128)} %get-tuple-element.17.refs_2_, ...), custom_call_target="tpu_custom_call" | custom-call | tf_op jit(solution)/shard_map/hand_out/pallas_call | solution.py:604
